TPU v7x, 512 devices: a whole 4x8x8 slice. The times are simulated.
512 devices in a mesh: ctx: 128 (over y, z, core), head: 4 (over x).
Axes of the slice: x: 4, y: 8, z: 8, core: 2. Of those that a mesh axis runs over, the one named last changes fastest.
Arguments:
- queries: bfloat16 [16384, 64, 576], P('ctx', 'head'), may hold values from -100 to 100
- latent_cache: bfloat16 [256, 36864], P('ctx'), may hold values from -6 to 6
- selected: int32 [256, 8], P('ctx'), may hold values from -1 to 255, as said below
- value_weight: bfloat16 [64, 512, 128], P('head'), may hold values from -0.25 to 0.25
Outputs:
- attended: bfloat16 [16384, 8192], P(('ctx', 'head'))
Inputs may be any that keep to these rules, and one draw needn't show every extreme that they name: `selected`: row b lists distinct key blocks: its first entry is b itself, the others lie below b; where b + 1 < 8 the row holds all of 0 to b and its remaining slots are -1.
All inputs are finite; a program needn't handle non-finite values.
Results may differ from a plain program's by a relative error of at most 0.011.
Values may be sent and summed in bfloat16 or wider, within the bound.
No kernel may reach another device: no remote copies, remote signals or barrier semaphores. Data moves between devices by JAX's collectives and lax.ppermute only.
A program may use at most 64 MiB of HBM per device.

v0:
```python
import jax
import jax.numpy as jnp
from jax import lax
from jax.sharding import PartitionSpec as P

DC = 512
DR = 64
DV = 128
KBLK = 64
SEL = 8


def attend_block(query_rows, key_rows, chosen_ids, block_index, value_weight):
    score_scale = (DV + DR) ** (-0.5)
    offsets = jnp.arange(KBLK, dtype=jnp.int32)
    valid_slot = chosen_ids >= 0
    clipped = jnp.maximum(chosen_ids, 0)
    key_place = (clipped[:, None] * KBLK + offsets[None, :]).reshape(-1)
    key_valid = jnp.repeat(valid_slot, KBLK)
    query_place = block_index * KBLK + offsets
    scores = (
        jnp.einsum("qhc,kc->hqk", query_rows, key_rows, preferred_element_type=jnp.float32)
        * score_scale
    )
    allowed = key_valid[None, None, :] & (key_place[None, None, :] <= query_place[None, :, None])
    scores = jnp.where(allowed, scores, -1e30)
    largest = jnp.max(scores, axis=2, keepdims=True)
    powered = jnp.exp(scores - largest)
    weights = (powered / jnp.sum(powered, axis=2, keepdims=True)).astype(jnp.bfloat16)
    mixed_latent = jnp.einsum(
        "hqk,kc->qhc", weights, key_rows[:, :DC], preferred_element_type=jnp.float32
    ).astype(jnp.bfloat16)
    expanded = jnp.einsum(
        "qhc,hcv->qhv", mixed_latent, value_weight, preferred_element_type=jnp.float32
    )
    return expanded.astype(jnp.bfloat16).reshape(KBLK, -1)


def per_device(queries, latent_cache, selected, value_weight):
    latent_width = DC + DR
    blocks_here = selected.shape[0]
    ctx_size = lax.axis_size("ctx")
    slice_width = latent_cache.shape[1] // ctx_size
    spread = lax.all_to_all(
        latent_cache.reshape(blocks_here, ctx_size, slice_width),
        "ctx",
        split_axis=1,
        concat_axis=0,
        tiled=True,
    )
    banded = spread.reshape(blocks_here * ctx_size, slice_width)
    every_choice = lax.all_gather(selected, "ctx", axis=0, tiled=True)
    clipped_all = jnp.maximum(every_choice, 0)
    pieces = banded[clipped_all].reshape(ctx_size, blocks_here, SEL, slice_width)
    fetched = lax.all_to_all(pieces, "ctx", split_axis=0, concat_axis=3, tiled=True)
    key_blocks = fetched.reshape(blocks_here, SEL * KBLK, latent_width)
    base_block = lax.axis_index("ctx") * blocks_here

    def one_block(position):
        query_rows = lax.dynamic_slice_in_dim(queries, position * KBLK, KBLK, 0)
        return attend_block(
            query_rows,
            key_blocks[position],
            selected[position],
            base_block + position,
            value_weight,
        )

    attended_here = lax.map(one_block, jnp.arange(blocks_here, dtype=jnp.int32))
    attended_here = attended_here.reshape(blocks_here * KBLK, -1)
    return lax.all_to_all(attended_here, "head", split_axis=0, concat_axis=1, tiled=True)


def solution(mesh):
    in_specs = (P("ctx", "head", None), P("ctx", None), P("ctx", None), P("head", None, None))
    out_specs = P(("ctx", "head"), None)
    return jax.shard_map(
        per_device, mesh=mesh, in_specs=in_specs, out_specs=out_specs, check_vma=False
    )
```

profile of v0, /device:TPU:1, one launch (start us, length us, event | category | flops | bytes accessed | tf_op | source)
XLA Modules:
  0.0 172.8 jit_solution(5769751596730198066)
XLA Ops:
  0.0 1.2 reshape.110
  1.2 0.9 copy.22
  2.1 18.4 %all-to-all-start = ((bf16[2,128,288]{2,0,1:T(2,128)(2,1)}), bf16[2,128,288]{2,0,1:T(2,128)(2,1)S(1)}, u32[]{:S(2)}, u32[]{:S(2)}) async-start(bf16[2,128,288]{2,0,1:T(2,128)(2,1)} %copy.22), calls=%async_computation | async-start | bytes 393216 | tf_op jit(solution)/shard_map/all_to_all | solution.py:44
  20.5 51.5 %all-gather = s32[128,2,8]{2,1,0:T(2,128)S(1)} all-gather(s32[1,2,8]{2,1,0:T(2,128)} %bitcast.70), channel_id=1, replica_groups=mesh['ctx'=128,'head'=4] {'ctx'}, dimensions={0}, use_global_device_ids=true | all-gather | bytes 8256 | tf_op jit(solution)/shard_map/all_gather | solution.py:52
  72.1 0.2 reshape.116
  72.3 0.2 reshape.111
  72.5 9.1 %gather_fusion = bf16[2048,288]{1,0:T(8,128)(2,1)} fusion(bf16[256,288]{1,0:T(8,128)(2,1)S(1)} %reshape.111, s32[2048]{0:T(1024)S(1)} %broadcast_clamp_fusion), kind=kCustom, calls=%fused_computation | custom fusion | bytes 2367488 | tf_op jit(solution)/shard_map/gather | solution.py:54
  81.6 9.7 %all-to-all-start.1 = ((bf16[128,2,8,288]{3,2,1,0:T(8,128)(2,1)}), bf16[128,2,8,288]{3,2,1,0:T(8,128)(2,1)S(1)}, u32[]{:S(2)}, u32[]{:S(2)}) async-start(bf16[128,2,8,288]{3,2,1,0:T(8,128)(2,1)} %bitcast.11), calls=%async_computation.1 | async-start | bytes 3145728 | tf_op jit(solution)/shard_map/all_to_all | solution.py:55
  91.3 4.3 %copy.25 = bf16[128,16,576]{2,0,1:T(8,128)(2,1)} copy(bf16[128,16,576]{0,2,1:T(8,128)(2,1)} %param.6) | data formatting | bytes 4718592 | tf_op jit(solution)/shard_map/while | solution.py:69
  95.6 36.8 %all-to-all-done.1 = bf16[128,2,8,288]{3,2,1,0:T(8,128)(2,1)S(1)} async-done(((bf16[128,2,8,288]{3,2,1,0:T(8,128)(2,1)}), bf16[128,2,8,288]{3,2,1,0:T(8,128)(2,1)S(1)}, u32[]{:S(2)}, u32[]{:S(2)}) %all-to-all-start.1) | async-done | bytes 1179680 | tf_op jit(solution)/shard_map/all_to_all | solution.py:55
  132.4 0.4 copy.23
  132.8 1.9 %reshape.113 = bf16[2,512,576]{2,1,0:T(8,128)(2,1)} reshape(bf16[1,2,8,128,288]{4,3,2,1,0:T(8,128)(2,1)S(1)} %copy.23) | data formatting | bytes 2359296 | tf_op jit(solution)/shard_map/reshape | solution.py:56
  134.7 1.6 copy.24
  136.3 23.8 %while.10 = (s32[]{:T(128)}, bf16[2,64,2048]{2,1,0:T(8,128)(2,1)S(1)}, s32[2]{0:T(128)S(1)}, bf16[2,512,576]{1,2,0:T(8,128)(2,1)S(1)}, s32[2,8]{1,0:T(2,128)S(1)...) while((s32[]{:T(128)}, ...), condition=%wide.region_3.4_spmd, body=%wide.region_0.3_spmd.sunk | while | flops 1278936192 | bytes 11819933 | solution.py:69
  136.4 0.6 dynamic_slice.52
  139.0 0.1 add.67
  139.1 0.1 and.23
  139.9 0.1 compare_and_fusion.2
  140.6 4.0 %fusion.43 = (f32[16,64]{1,0:T(8,128)S(1)}, f32[16,64,512]{2,1,0:T(8,128)}) fusion(pred[64,512]{1,0:T(8,128)(4,1)S(1)} %compare_and_fusion.2, bf16[128,16,576]{2,0,1:T(8,128)(2,1)} %get-tuple-element.183, s32[]{:T(128)S(6)} %select_n.23, bf16[2,512,576]{1,2,0:T(8,128)(2,1)S(1)} %get-tuple-element.180, s32[]{:T(128)S(6)} %select_n.22), kind=kOutput, calls=%fused_computation.32.clone.1 | convolution fusion | flops 606077440 | bytes 4034568 | tf_op jit(solution)/shard_map/while/body/eval_jaxpr/sub | solution.py:28
  144.6 3.3 %fusion.44 = bf16[64,16,128]{2,0,1:T(8,128)(2,1)S(1)} fusion(bf16[16,512,128]{2,1,0:T(8,128)(2,1)} %get-tuple-element.184, f32[16,64,512]{2,1,0:T(8,128)} %get-tuple-element.149, f32[16,64]{1,0:T(8,128)S(1)} %get-tuple-element.150, bf16[512,576]{0,1:T(8,128)(2,1)S(1)} %dynamic-slice_bitcast_fusion.2), kind=kOutput, calls=%fused_computation.11.clone.1 | convolution fusion | flops 672792576 | bytes 4988928 | tf_op jit(solution)/shard_map/while/body/eval_jaxpr/qhc,hcv->qhv/dot_general | solution.py:33
  147.9 0.2 copy.31
  148.1 0.1 broadcast_in_dim.53
  148.3 0.6 dynamic_slice.52
  150.9 0.1 add.67
  151.1 0.1 and.23
  151.8 0.1 compare_and_fusion.2
  152.6 4.0 %fusion.43 = (f32[16,64]{1,0:T(8,128)S(1)}, f32[16,64,512]{2,1,0:T(8,128)}) fusion(pred[64,512]{1,0:T(8,128)(4,1)S(1)} %compare_and_fusion.2, bf16[128,16,576]{2,0,1:T(8,128)(2,1)} %get-tuple-element.183, s32[]{:T(128)S(6)} %select_n.23, bf16[2,512,576]{1,2,0:T(8,128)(2,1)S(1)} %get-tuple-element.180, s32[]{:T(128)S(6)} %select_n.22), kind=kOutput, calls=%fused_computation.32.clone.1 | convolution fusion | flops 606077440 | bytes 4034568 | tf_op jit(solution)/shard_map/while/body/eval_jaxpr/sub | solution.py:28
  156.6 3.3 %fusion.44 = bf16[64,16,128]{2,0,1:T(8,128)(2,1)S(1)} fusion(bf16[16,512,128]{2,1,0:T(8,128)(2,1)} %get-tuple-element.184, f32[16,64,512]{2,1,0:T(8,128)} %get-tuple-element.149, f32[16,64]{1,0:T(8,128)S(1)} %get-tuple-element.150, bf16[512,576]{0,1:T(8,128)(2,1)S(1)} %dynamic-slice_bitcast_fusion.2), kind=kOutput, calls=%fused_computation.11.clone.1 | convolution fusion | flops 672792576 | bytes 4988928 | tf_op jit(solution)/shard_map/while/body/eval_jaxpr/qhc,hcv->qhv/dot_general | solution.py:33
  159.8 0.2 copy.31
  160.0 0.1 broadcast_in_dim.53
  160.2 11.7 %all_to_all.49 = bf16[4,32,2048]{2,1,0:T(8,128)(2,1)S(1)} all-to-all(bf16[4,32,2048]{2,1,0:T(8,128)(2,1)S(1)} %bitcast.69), channel_id=1, replica_groups=mesh['ctx'=128,'head'=4] {'head'}, dimensions={0} | all-to-all | bytes 1048576 | tf_op jit(solution)/shard_map/all_to_all | solution.py:71
  171.9 0.8 copy.29
  (23 shorter events, 0.6 us)
Async XLA Ops:
  2.1 70.2 %all-to-all-start = ((bf16[2,128,288]{2,0,1:T(2,128)(2,1)}), bf16[2,128,288]{2,0,1:T(2,128)(2,1)S(1)}, u32[]{:S(2)}, u32[]{:S(2)}) async-start(bf16[2,128,288]{2,0,1:T(2,128)(2,1)} %copy.22), calls=%async_computation | async-start | bytes 393216 | tf_op jit(solution)/shard_map/all_to_all | solution.py:44
  81.6 50.8 %all-to-all-start.1 = ((bf16[128,2,8,288]{3,2,1,0:T(8,128)(2,1)}), bf16[128,2,8,288]{3,2,1,0:T(8,128)(2,1)S(1)}, u32[]{:S(2)}, u32[]{:S(2)}) async-start(bf16[128,2,8,288]{3,2,1,0:T(8,128)(2,1)} %bitcast.11), calls=%async_computation.1 | async-start | bytes 3145728 | tf_op jit(solution)/shard_map/all_to_all | solution.py:55
  132.8 3.6 %copy-start.1 = (s32[2,8]{1,0:T(2,128)S(1)}, s32[2,8]{1,0:T(2,128)}, u32[]{:S(2)}) copy-start(s32[2,8]{1,0:T(2,128)} %param.8) | copy-start | bytes 196
  134.7 1.7 copy-start
where the time goes:
time: 174 us; the launch traced here: 173 us
  blocking collectives  63.2 us (36%)
  waiting for transfers between devices  36.8 us (21%)
  starting transfers between devices  28.1 us (16%)
  local copies, waits for them, and re-layouts  23 us (13%)
  matrix products  14.5 us (8%)
  loops' own time  6.64 us (4%)
    all_gather x1, blocking collectives, per_device(): every_choice = lax.all_gather(selected, 'ctx', axis=0, tiled=True)  51.5 us
    all_to_all x1, waiting for transfers between devices, per_device(): lax.all_to_all(pieces, 'ctx', split_axis=0, concat_axis=3, tiled=True)  36.8 us
    all_to_all x1, starting transfers between devices, per_device(): lax.all_to_all(latent_cache.reshape(blocks_here, ctx_size, slice_width),...  18.4 us
    all_to_all x1, blocking collectives, per_device(): lax.all_to_all(attended_here, 'head', split_axis=0, concat_axis=1, tiled=...  11.7 us
    all_to_all x1, starting transfers between devices, per_device(): lax.all_to_all(pieces, 'ctx', split_axis=0, concat_axis=3, tiled=True)  9.7 us
    gather x1, local copies, waits for them, and re-layouts, per_device(): banded[clipped_all].reshape(ctx_size, blocks_here, SEL, slice_width)  9.09 us
    sub x2, matrix products, attend_block(): powered = jnp.exp(scores - largest)  7.93 us
    another operation x1, loops' own time, per_device(): attended_here = lax.map(one_block, jnp.arange(blocks_here, dtype=jnp.int32))  6.64 us
  transfers between devices with their start and end apart: 2, of which 1 were waited for; matrix products, arithmetic and copies ran while one was open for 3% of the time, Pallas kernels for 0%

commit v1 on v0

v1 whole, which is shorter than its diff:
```python
import functools

import jax
import jax.numpy as jnp
from jax import lax
from jax.experimental import pallas as pl
from jax.experimental.pallas import tpu as pltpu
from jax.sharding import PartitionSpec as P

DC = 512
DR = 64
DV = 128
KBLK = 64
SEL = 8
WIDTH = DC + DR
ROW = 640
GROUP = 16
HEAD_BLOCK = 4


def attend_kernel(base_ref, q_ref, k_ref, kpos_ref, w_ref, o_ref):
    heads, rows, width = q_ref.shape
    keys = k_ref[...]
    block = pl.program_id(0)
    queries = q_ref[...].reshape(heads * rows, width)
    scores = lax.dot_general(
        queries, keys, (((1,), (1,)), ((), ())), preferred_element_type=jnp.float32
    ) * ((DV + DR) ** -0.5)
    first = (base_ref[0] + block) * KBLK
    query_place = first + lax.broadcasted_iota(jnp.int32, (rows, 1), 0)
    allowed = kpos_ref[0] <= query_place
    scores = scores.reshape(heads, rows, -1)
    scores = jnp.where(allowed[None], scores, -1e30)
    largest = jnp.max(scores, axis=2, keepdims=True)
    powered = jnp.exp(scores - largest)
    weights = (powered / jnp.sum(powered, axis=2, keepdims=True)).astype(jnp.bfloat16)
    mixed = lax.dot_general(
        weights.reshape(heads * rows, -1),
        keys[:, :DC],
        (((1,), (0,)), ((), ())),
        preferred_element_type=jnp.float32,
    ).astype(jnp.bfloat16)
    for head in range(heads):
        expanded = jnp.dot(
            mixed[head * rows : (head + 1) * rows], w_ref[head], preferred_element_type=jnp.float32
        )
        o_ref[:, head * DV : (head + 1) * DV] = expanded.astype(jnp.bfloat16)


def attend(base, queries, keys, key_place, value_weight):
    heads, tokens, width = queries.shape
    blocks = tokens // KBLK
    count = keys.shape[1]
    return pl.pallas_call(
        attend_kernel,
        out_shape=jax.ShapeDtypeStruct((tokens, heads * DV), jnp.bfloat16),
        grid_spec=pltpu.PrefetchScalarGridSpec(
            num_scalar_prefetch=1,
            grid=(blocks, heads // HEAD_BLOCK),
            in_specs=[
                pl.BlockSpec((HEAD_BLOCK, KBLK, width), lambda b, h, base: (h, b, 0)),
                pl.BlockSpec((None, count, width), lambda b, h, base: (b, 0, 0)),
                pl.BlockSpec((1, 1, count), lambda b, h, base: (b, 0, 0)),
                pl.BlockSpec((HEAD_BLOCK, DC, DV), lambda b, h, base: (h, 0, 0)),
            ],
            out_specs=pl.BlockSpec((KBLK, HEAD_BLOCK * DV), lambda b, h, base: (b, h)),
        ),
    )(base, queries, keys, key_place, value_weight)


def per_device(queries, latent_cache, selected, value_weight):
    ctx_size = lax.axis_size("ctx")
    head_size = lax.axis_size("head")
    ctx = lax.axis_index("ctx")
    head = lax.axis_index("head")
    here = selected.shape[0]
    rows = ctx_size // GROUP
    groups = [[row * GROUP + i for i in range(GROUP)] for row in range(rows)]

    cache = latent_cache.reshape(here, KBLK, WIDTH)
    mine = lax.dynamic_slice_in_dim(cache, head * GROUP, GROUP, 1)
    lists = jnp.broadcast_to(selected.astype(jnp.bfloat16)[:, None, :], (here, GROUP, SEL))
    filler = jnp.zeros((here, GROUP, ROW - WIDTH - SEL), jnp.bfloat16)
    mine = jnp.concatenate([mine, lists, filler], axis=2).transpose(1, 0, 2)
    spread = lax.all_to_all(
        jnp.broadcast_to(mine[None], (rows, GROUP, here, ROW)).reshape(ctx_size, here, ROW),
        "ctx", split_axis=0, concat_axis=0, tiled=True,
    )
    table = spread.reshape(ctx_size * here, ROW)
    near = lax.dynamic_slice_in_dim(table, (ctx // GROUP) * GROUP * here, GROUP * here, 0)
    wanted = near[:, WIDTH : WIDTH + SEL].astype(jnp.int32).reshape(-1)
    chosen = wanted[:, None] == jnp.arange(ctx_size * here, dtype=jnp.int32)[None, :]
    picked = jnp.dot(
        chosen.astype(jnp.bfloat16), table[:, :WIDTH], preferred_element_type=jnp.float32
    ).astype(jnp.bfloat16)

    fetched = lax.all_to_all(
        picked.reshape(GROUP, here, SEL, WIDTH), "ctx", split_axis=0, concat_axis=0,
        axis_index_groups=groups, tiled=True,
    )
    shared = lax.all_to_all(
        jnp.broadcast_to(fetched[None], (head_size, GROUP, here, SEL, WIDTH)),
        "head", split_axis=0, concat_axis=0, tiled=True,
    )
    keys = shared.reshape(KBLK, here, SEL, WIDTH).transpose(1, 0, 2, 3).reshape(here, KBLK * SEL, WIDTH)

    offsets = jnp.arange(KBLK, dtype=jnp.int32)
    place = jnp.where(selected[:, None, :] >= 0, selected[:, None, :] * KBLK + offsets[None, :, None], 2**30)
    place = place.reshape(here, 1, KBLK * SEL)
    base = (ctx * here).astype(jnp.int32).reshape(1)
    attended = attend(base, queries.transpose(1, 0, 2), keys, place, value_weight)
    return lax.all_to_all(attended, "head", split_axis=0, concat_axis=1, tiled=True)


def solution(mesh):
    in_specs = (P("ctx", "head", None), P("ctx", None), P("ctx", None), P("head", None, None))
    out_specs = P(("ctx", "head"), None)
    return jax.shard_map(
        per_device, mesh=mesh, in_specs=in_specs, out_specs=out_specs, check_vma=False
    )
```

time: 174 us -> 105 us (0.60)
  blocking collectives: 63.2 us -> 30.2 us
  matrix products: 14.5 us -> 0.35 us
  local copies, waits for them, and re-layouts: 23 us -> 10.6 us
  Pallas kernels: 0 us -> 10.6 us
  waiting for transfers between devices: 36.8 us -> 28.6 us
  loops' own time: 6.64 us -> 0 us
  starting transfers between devices: 28.1 us -> 22.5 us
    all_gather x1 -> x0, blocking collectives: 51.5 us -> none  [per_device(): every_choice = lax.all_gather(selected, 'ctx', axis=0, tiled=True)]
    all_to_all x1 -> x2, blocking collectives: 11.7 us -> 30.2 us  [the longest x1 17.6 us: per_device(): lax.all_to_all(picked.reshape(GROUP, here, SEL, WIDTH), 'ctx', split_axis...]
    pallas_call x0 -> x1, Pallas kernels: none -> 10.6 us  [attend(): pl.pallas_call(attend_kernel, out_shape=jax.ShapeDtypeStruct((tokens, hea...]
    gather x1 -> x0, local copies, waits for them, and re-layouts: 9.09 us -> none  [per_device(): banded[clipped_all].reshape(ctx_size, blocks_here, SEL, slice_width)]
    all_to_all x2, waiting for transfers between devices: 36.8 us -> 28.6 us  [the longest x1 15.5 us: per_device(): lax.all_to_all(jnp.broadcast_to(mine[None], (rows, GROUP, here, ROW)).res...]
    sub x2 -> x0, matrix products: 7.93 us -> none  [attend_block(): powered = jnp.exp(scores - largest)]
    another operation x1 -> x0, loops' own time: 6.64 us -> none  [per_device(): attended_here = lax.map(one_block, jnp.arange(blocks_here, dtype=jnp.int32))]
    dot_general x2 -> x1, matrix products: 6.55 us -> 0.35 us  [per_device(): jnp.dot(chosen.astype(jnp.bfloat16), table[:, :WIDTH], preferred_element_...]
  transfers between devices with their start and end apart: 2 -> 2, of which waited for: 1 -> 2; matrix products, arithmetic and copies ran while one was open for 3% -> 5% of each run, Pallas kernels for 0% -> 0%
where the time goes in v1:
time: 105 us
  blocking collectives  30.2 us (29%)
  waiting for transfers between devices  28.6 us (27%)
  starting transfers between devices  22.5 us (21%)
  local copies, waits for them, and re-layouts  10.6 us (10%)
  Pallas kernels  10.6 us (10%)
  other arithmetic  1.54 us (1%)
    all_to_all x1, starting transfers between devices, per_device(): lax.all_to_all(jnp.broadcast_to(mine[None], (rows, GROUP, here, ROW)).res...  18.4 us
    all_to_all x1, blocking collectives, per_device(): lax.all_to_all(picked.reshape(GROUP, here, SEL, WIDTH), 'ctx', split_axis...  17.6 us
    all_to_all x1, waiting for transfers between devices, per_device(): lax.all_to_all(jnp.broadcast_to(mine[None], (rows, GROUP, here, ROW)).res...  15.5 us
    all_to_all x1, waiting for transfers between devices, per_device(): lax.all_to_all(jnp.broadcast_to(fetched[None], (head_size, GROUP, here, S...  13.1 us
    all_to_all x1, blocking collectives, per_device(): lax.all_to_all(attended, 'head', split_axis=0, concat_axis=1, tiled=True)  12.6 us
    pallas_call x1, Pallas kernels, attend(): pl.pallas_call(attend_kernel, out_shape=jax.ShapeDtypeStruct((tokens, hea...  10.6 us
    unnamed x3, local copies, waits for them, and re-layouts  4.33 us
    all_to_all x1, starting transfers between devices, per_device(): lax.all_to_all(jnp.broadcast_to(fetched[None], (head_size, GROUP, here, S...  4.14 us
  transfers between devices with their start and end apart: 2, of which 2 were waited for; matrix products, arithmetic and copies ran while one was open for 5% of the time, Pallas kernels for 0%

profile of v1, /device:TPU:1, one launch (start us, length us, event | category | flops | bytes accessed | tf_op | source)
XLA Modules:
  0.0 104.5 jit_solution(15054053035201025805)
XLA Ops:
  0.0 0.8 broadcast_multiply_fusion
  0.8 1.1 %reshape.80 = bf16[2,64,576]{2,1,0:T(8,128)(2,1)S(1)} reshape(bf16[2,36864]{1,0:T(2,128)(2,1)} %param.5) | data formatting | bytes 294912 | tf_op jit(solution)/shard_map/reshape | solution.py:80
  1.9 0.1 pad.2.clone
  2.0 0.1 maximum_bitcast_fusion
  2.1 0.9 broadcast_in_dim.20
  3.0 18.4 %all-to-all-start = ((bf16[128,2,640]{2,1,0:T(2,128)(2,1)}), bf16[128,2,640]{2,1,0:T(2,128)(2,1)S(1)}, u32[]{:S(2)}, u32[]{:S(2)}) async-start(bf16[128,2,640]{2,1,0:T(2,128)(2,1)} %bitcast.3), calls=%async_computation | async-start | bytes 655360 | tf_op jit(solution)/shard_map/all_to_all | solution.py:85
  21.4 15.5 %all-to-all-done = bf16[128,2,640]{2,1,0:T(2,128)(2,1)S(1)} async-done(((bf16[128,2,640]{2,1,0:T(2,128)(2,1)}), bf16[128,2,640]{2,1,0:T(2,128)(2,1)S(1)}, u32[]{:S(2)}, u32[]{:S(2)}) %all-to-all-start) | async-done | bytes 327712 | tf_op jit(solution)/shard_map/all_to_all | solution.py:85
  36.9 0.1 reshape.82
  37.0 0.1 dynamic-slice_convert_fusion
  37.1 0.1 reshape.86
  37.2 0.4 convolution_convert_fusion
  37.6 0.2 copy.25
  37.8 17.6 %all_to_all.34 = bf16[16,2,8,576]{3,2,1,0:T(8,128)(2,1)S(1)} all-to-all(bf16[16,2,8,576]{3,2,1,0:T(8,128)(2,1)S(1)} %bitcast.20), channel_id=1, replica_groups={{0,4,8,12,16,20,24,28,32,36,40,44,48,52,56,60},{64,68,72,76,80,84,88,92..., dimensions={0} | all-to-all | bytes 589824 | tf_op jit(solution)/shard_map/all_to_all | solution.py:97
  55.4 1.2 %broadcast_in_dim.42 = bf16[4,16,2,8,576]{4,3,1,2,0:T(8,128)(2,1)} broadcast(bf16[16,2,8,576]{3,2,0,1:T(8,128)(2,1)S(1)} %copy.26), dimensions={1,2,3,4} | broadcast | bytes 1474560 | tf_op jit(solution)/shard_map/broadcast_in_dim | solution.py:102
  56.6 0.0 copy-start
  56.6 4.1 %all-to-all-start.2 = ((bf16[4,16,2,8,576]{4,3,1,2,0:T(8,128)(2,1)}), bf16[4,16,2,8,576]{4,3,1,2,0:T(8,128)(2,1)S(1)}, u32[]{:S(2)}, u32[]{:S(2)}) async-start(bf16[4,16,2,8,576]{4,3,1,2,0:T(8,128)(2,1)} %broadcast_in_dim.42), calls=%async_computation.2 | async-start | bytes 2621440 | tf_op jit(solution)/shard_map/all_to_all | solution.py:101
  60.7 0.0 copy-done
  60.7 0.1 broadcast_in_dim.46
  60.8 0.1 add.38
  60.9 0.1 add.41
  61.0 4.3 %copy.23 = bf16[128,16,576]{2,0,1:T(8,128)(2,1)} copy(bf16[128,16,576]{0,2,1:T(8,128)(2,1)} %param.4) | data formatting | bytes 4718592 | tf_op args[0]
  65.4 0.6 add_select_fusion.kpos_ref
  66.0 13.1 %all-to-all-done.2 = bf16[4,16,2,8,576]{4,3,1,2,0:T(8,128)(2,1)S(1)} async-done(((bf16[4,16,2,8,576]{4,3,1,2,0:T(8,128)(2,1)}), bf16[4,16,2,8,576]{4,3,1,2,0:T(8,128)(2,1)S(1)}, u32[]{:S(2)}, u32[]{:S(2)}) %all-to-all-start.2) | async-done | bytes 1179680 | tf_op jit(solution)/shard_map/all_to_all | solution.py:101
  79.0 0.1 copy.27
  79.2 1.3 %copy_bitcast_fusion.k_ref = bf16[2,512,576]{2,1,0:T(8,128)(2,1)} fusion(bf16[4,16,2,8,576]{4,3,2,1,0:T(8,128)(2,1)S(1)} %copy.27), kind=kLoop, calls=%fused_computation | loop fusion | bytes 2359296 | tf_op jit(solution)/shard_map/reshape | solution.py:105
  80.4 10.6 %shard_map.46 = bf16[128,2048]{1,0:T(8,128)(2,1)} custom-call(s32[1]{0:T(128)} %bitcast.base_ref, bf16[16,128,576]{2,1,0:T(8,128)(2,1)} %bitcast.17, bf16[2,512,576]{2,1,0:T(8,128)(2,1)} %copy_bitcast_fusion.k_ref, s32[2,1,512]{2,1,0:T(1,128)} %add_select_fusion.kpos_ref, bf16[16,512,128]{2,1,0:T(8,128)(2,1)} %w_ref.1), custom_call_target="tpu_custom_call" | custom-call | tf_op jit(solution)/shard_map/pallas_call | solution.py:54
  91.1 12.6 %all_to_all.35 = bf16[4,32,2048]{2,1,0:T(8,128)(2,1)S(1)} all-to-all(bf16[4,32,2048]{2,1,0:T(8,128)(2,1)} %bitcast.18), channel_id=1, replica_groups=mesh['ctx'=128,'head'=4] {'head'}, dimensions={0} | all-to-all | bytes 1048576 | tf_op jit(solution)/shard_map/all_to_all | solution.py:112
  103.7 0.8 copy.32
  (9 shorter events, 0.1 us)
Async XLA Ops:
  3.0 33.9 %all-to-all-start = ((bf16[128,2,640]{2,1,0:T(2,128)(2,1)}), bf16[128,2,640]{2,1,0:T(2,128)(2,1)S(1)}, u32[]{:S(2)}, u32[]{:S(2)}) async-start(bf16[128,2,640]{2,1,0:T(2,128)(2,1)} %bitcast.3), calls=%async_computation | async-start | bytes 655360 | tf_op jit(solution)/shard_map/all_to_all | solution.py:85
  56.6 4.1 %copy-start = (s32[2,8]{1,0:T(2,128)S(1)}, s32[2,8]{1,0:T(2,128)}, u32[]{:S(2)}) copy-start(s32[2,8]{1,0:T(2,128)} %param.6) | copy-start | bytes 196
  56.6 22.5 %all-to-all-start.2 = ((bf16[4,16,2,8,576]{4,3,1,2,0:T(8,128)(2,1)}), bf16[4,16,2,8,576]{4,3,1,2,0:T(8,128)(2,1)S(1)}, u32[]{:S(2)}, u32[]{:S(2)}) async-start(bf16[4,16,2,8,576]{4,3,1,2,0:T(8,128)(2,1)} %broadcast_in_dim.42), calls=%async_computation.2 | async-start | bytes 2621440 | tf_op jit(solution)/shard_map/all_to_all | solution.py:101

commit v2 on v1

v2 whole, which is shorter than its diff:
```python
import jax
import jax.numpy as jnp
from jax import lax
from jax.experimental import pallas as pl
from jax.experimental.pallas import tpu as pltpu
from jax.sharding import PartitionSpec as P

DC = 512
DR = 64
DV = 128
KBLK = 64
SEL = 8
WIDTH = DC + DR
BAND_TOKENS = 2
BAND = BAND_TOKENS * WIDTH
ROW = BAND + 128
Y, Z, CORES = 8, 8, 2
HEAD_BLOCK = 8
FACTOR = (DV + DR) ** -0.5 * 1.4426950408889634


def attend_kernel(base_ref, q_ref, k_ref, place_ref, w_ref, o_ref, keys_ref, bias_ref):
    heads, tokens, width = q_ref.shape
    bands, per_band, _ = k_ref.shape
    blocks = tokens // KBLK
    slots = per_band // blocks
    half = bands * slots

    @pl.when(pl.program_id(0) == 0)
    def _():
        for block in range(blocks):
            picked = slice(block * slots, (block + 1) * slots)
            for token in range(BAND_TOKENS):
                rows = k_ref[:, picked, token * width : (token + 1) * width]
                keys_ref[block, token * half : (token + 1) * half, :] = rows.reshape(half, width)
            first = (base_ref[0] + block) * KBLK
            query_place = first + lax.broadcasted_iota(jnp.int32, (KBLK, 1), 0)
            bias_ref[block] = jnp.where(place_ref[block] <= query_place, 0.0, -1e30)

    for block in range(blocks):
        keys = keys_ref[block]
        here = slice(block * KBLK, (block + 1) * KBLK)
        queries = q_ref[:, here, :].reshape(heads * KBLK, width)
        scores = lax.dot_general(
            queries, keys, (((1,), (1,)), ((), ())), preferred_element_type=jnp.float32
        )
        scores = scores.reshape(heads, KBLK, -1) * FACTOR + bias_ref[block][None]
        powered = jnp.exp2(scores - jnp.max(scores, axis=2, keepdims=True))
        total = jnp.sum(powered, axis=2, keepdims=True)
        mixed = lax.dot_general(
            powered.astype(jnp.bfloat16).reshape(heads * KBLK, -1),
            keys[:, :DC],
            (((1,), (0,)), ((), ())),
            preferred_element_type=jnp.float32,
        ).astype(jnp.bfloat16)
        for head in range(heads):
            expanded = jnp.dot(
                mixed[head * KBLK : (head + 1) * KBLK],
                w_ref[head],
                preferred_element_type=jnp.float32,
            )
            o_ref[here, head * DV : (head + 1) * DV] = (expanded / total[head]).astype(jnp.bfloat16)


def attend(base, queries, keys, place, value_weight):
    heads, tokens, width = queries.shape
    blocks, _, count = place.shape
    return pl.pallas_call(
        attend_kernel,
        out_shape=jax.ShapeDtypeStruct((tokens, heads * DV), jnp.bfloat16),
        grid_spec=pltpu.PrefetchScalarGridSpec(
            num_scalar_prefetch=1,
            grid=(heads // HEAD_BLOCK,),
            in_specs=[
                pl.BlockSpec((HEAD_BLOCK, tokens, width), lambda h, base: (h, 0, 0)),
                pl.BlockSpec(keys.shape, lambda h, base: (0, 0, 0)),
                pl.BlockSpec(place.shape, lambda h, base: (0, 0, 0)),
                pl.BlockSpec((HEAD_BLOCK, DC, DV), lambda h, base: (h, 0, 0)),
            ],
            out_specs=pl.BlockSpec((tokens, HEAD_BLOCK * DV), lambda h, base: (0, h)),
            scratch_shapes=[
                pltpu.VMEM((blocks, count, width), jnp.bfloat16),
                pltpu.VMEM((blocks, KBLK, count), jnp.float32),
            ],
        ),
    )(base, queries, keys, place, value_weight)


def fetch_groups(heads):
    groups = []
    for y in range(Y // 2):
        for z in range(Z // 2):
            groups.append([
                (((2 * y + dy) * Z + 2 * z + dz) * CORES + core) * heads + head
                for head in range(heads)
                for dy in range(2)
                for dz in range(2)
                for core in range(CORES)
            ])
    return groups


def per_device(queries, latent_cache, selected, value_weight):
    ctx_size = lax.axis_size("ctx")
    heads = lax.axis_size("head")
    ctx = lax.axis_index("ctx")
    head = lax.axis_index("head")
    here = selected.shape[0]
    cell = 4 * CORES
    bands = heads * cell

    mine = latent_cache.reshape(here, bands, BAND)
    mine = lax.dynamic_slice_in_dim(mine, head * cell, cell, 1).transpose(1, 0, 2)
    lists = jnp.broadcast_to(selected.astype(jnp.bfloat16), (cell, here, SEL))
    filler = jnp.zeros((cell, here, ROW - BAND - SEL), jnp.bfloat16)
    mine = jnp.concatenate([mine, lists, filler], axis=2).reshape(1, 2, 1, 2, CORES, here, ROW)
    spread = lax.all_to_all(
        jnp.broadcast_to(mine, (Y // 2, 2, Z // 2, 2, CORES, here, ROW)).reshape(ctx_size, here, ROW),
        "ctx",
        split_axis=0,
        concat_axis=0,
        tiled=True,
    )
    table = spread.reshape(ctx_size * here, ROW)

    lists = spread[:, :, BAND : BAND + SEL].reshape(Y // 2, 2, Z // 2, 2, CORES, here, SEL)
    y, z = ctx // (Z * CORES), (ctx // CORES) % Z
    lists = lax.dynamic_slice_in_dim(lists, y // 2, 1, 0)
    lists = lax.dynamic_slice_in_dim(lists, z // 2, 1, 2)
    wanted = lists.astype(jnp.int32).reshape(-1)
    chosen = wanted[:, None] == jnp.arange(ctx_size * here, dtype=jnp.int32)[None, :]
    picked = jnp.dot(
        chosen.astype(jnp.bfloat16), table[:, :BAND], preferred_element_type=jnp.float32
    ).astype(jnp.bfloat16)
    picked = picked.reshape(1, cell, here * SEL, BAND)
    keys = lax.all_to_all(
        jnp.broadcast_to(picked, (heads, cell, here * SEL, BAND)).reshape(bands, here * SEL, BAND),
        ("ctx", "head"),
        split_axis=0,
        concat_axis=0,
        axis_index_groups=fetch_groups(heads),
        tiled=True,
    )

    offsets = (
        jnp.arange(BAND_TOKENS, dtype=jnp.int32)[:, None]
        + BAND_TOKENS * jnp.arange(bands, dtype=jnp.int32)[None, :]
    )
    place = selected[:, None, None, :] * KBLK + offsets[None, :, :, None]
    place = jnp.where(selected[:, None, None, :] >= 0, place, 2**30)
    place = place.reshape(here, 1, SEL * KBLK)
    base = (ctx * here).astype(jnp.int32).reshape(1)
    attended = attend(base, queries.transpose(1, 0, 2), keys, place, value_weight)
    return lax.all_to_all(attended, "head", split_axis=0, concat_axis=1, tiled=True)


def solution(mesh):
    in_specs = (P("ctx", "head", None), P("ctx", None), P("ctx", None), P("head", None, None))
    out_specs = P(("ctx", "head"), None)
    return jax.shard_map(
        per_device, mesh=mesh, in_specs=in_specs, out_specs=out_specs, check_vma=False
    )
```

time: 105 us -> 93.7 us (0.89)
  blocking collectives: 30.2 us -> 12.8 us
  waiting for transfers between devices: 28.6 us -> 32.5 us
  Pallas kernels: 10.6 us -> 7.3 us
  starting transfers between devices: 22.5 us -> 25.4 us
  local copies, waits for them, and re-layouts: 10.6 us -> 12.7 us
    all_to_all x1 -> x0, blocking collectives: 17.6 us -> none  [per_device(): lax.all_to_all(picked.reshape(GROUP, here, SEL, WIDTH), 'ctx', split_axis...]
    all_to_all x2, waiting for transfers between devices: 28.6 us -> 32.5 us  [the longest x1 22.1 us: per_device(): lax.all_to_all(jnp.broadcast_to(mine, (Y // 2, 2, Z // 2, 2, CORES, here,...]
    add x4, local copies, waits for them, and re-layouts: 0.2 us -> 3.77 us  [per_device(): place = selected[:, None, None, :] * KBLK + offsets[None, :, :, None]]
    pallas_call x1, Pallas kernels: 10.6 us -> 7.3 us  [attend(): pl.pallas_call(attend_kernel, out_shape=jax.ShapeDtypeStruct((tokens, hea...]
    all_to_all x2, starting transfers between devices: 22.5 us -> 25.4 us  [the longest x1 18.4 us: per_device(): lax.all_to_all(jnp.broadcast_to(mine, (Y // 2, 2, Z // 2, 2, CORES, here,...]
    reshape x2 -> x0, local copies, waits for them, and re-layouts: 2.38 us -> none  [the longest x1 1.28 us: per_device(): shared.reshape(KBLK, here, SEL, WIDTH).transpose(1, 0, 2, 3)]
    broadcast_in_dim x6 -> x7, local copies, waits for them, and re-layouts: 2.17 us -> 3.04 us  [the longest x2 1.21 us: per_device(): jnp.broadcast_to(mine, (Y // 2, 2, Z // 2, 2, CORES, here, ROW))]
    unnamed x3 -> x11, local copies, waits for them, and re-layouts: 4.33 us -> 4.56 us
  transfers between devices with their start and end apart: 2 -> 2, of which waited for: 2 -> 2; matrix products, arithmetic and copies ran while one was open for 5% -> 8% of each run, Pallas kernels for 0% -> 0%
where the time goes in v2:
time: 93.7 us; the launch traced here: 93.2 us
  waiting for transfers between devices  32.5 us (35%)
  starting transfers between devices  25.4 us (27%)
  blocking collectives  12.8 us (14%)
  local copies, waits for them, and re-layouts  12.7 us (14%)
  Pallas kernels  7.3 us (8%)
  other arithmetic  1.96 us (2%)
    all_to_all x1, waiting for transfers between devices, per_device(): lax.all_to_all(jnp.broadcast_to(mine, (Y // 2, 2, Z // 2, 2, CORES, here,...  22.1 us
    all_to_all x1, starting transfers between devices, per_device(): lax.all_to_all(jnp.broadcast_to(mine, (Y // 2, 2, Z // 2, 2, CORES, here,...  18.4 us
    all_to_all x1, blocking collectives, per_device(): lax.all_to_all(attended, 'head', split_axis=0, concat_axis=1, tiled=True)  12.8 us
    all_to_all x1, waiting for transfers between devices, per_device(): lax.all_to_all(jnp.broadcast_to(picked, (heads, cell, here * SEL, BAND))....  10.4 us
    pallas_call x1, Pallas kernels, attend(): pl.pallas_call(attend_kernel, out_shape=jax.ShapeDtypeStruct((tokens, hea...  7.3 us
    all_to_all x1, starting transfers between devices, per_device(): lax.all_to_all(jnp.broadcast_to(picked, (heads, cell, here * SEL, BAND))....  6.96 us
    unnamed x11, local copies, waits for them, and re-layouts  4.56 us
    add x4, local copies, waits for them, and re-layouts, per_device(): place = selected[:, None, None, :] * KBLK + offsets[None, :, :, None]  3.77 us
  transfers between devices with their start and end apart: 2, of which 2 were waited for; matrix products, arithmetic and copies ran while one was open for 8% of the time, Pallas kernels for 0%

profile of v2, /device:TPU:1, one launch (start us, length us, event | category | flops | bytes accessed | tf_op | source)
XLA Modules:
  0.0 93.2 jit_solution(2365319335072348549)
XLA Ops:
  0.0 1.3 %broadcast_multiply_fusion = (s32[2,8]{1,0:T(2,128)}, bf16[2,8]{1,0:T(2,128)(2,1)S(1)}) fusion(s32[2,8]{1,0:T(2,128)} %param.6), kind=kLoop, calls=%fused_computation.10 | loop fusion | flops 32 | bytes 160 | tf_op jit(solution)/shard_map/mul | solution.py:149
  1.3 0.9 copy.31
  2.3 0.1 concatenate.3
  2.4 1.2 %broadcast_in_dim.43 = bf16[4,2,4,2,2,2,1280]{6,5,4,3,2,1,0:T(2,128)(2,1)} broadcast(bf16[2,2,2,2,1280]{4,3,2,1,0:T(2,128)(2,1)S(1)} %bitcast.28), dimensions={1,3,4,5,6} | broadcast | bytes 696320 | tf_op jit(solution)/shard_map/broadcast_in_dim | solution.py:118
  3.6 18.4 %all-to-all-start = ((bf16[128,2,1280]{2,1,0:T(2,128)(2,1)}), bf16[128,2,1280]{2,1,0:T(2,128)(2,1)S(1)}, u32[]{:S(2)}, u32[]{:S(2)}) async-start(bf16[128,2,1280]{2,1,0:T(2,128)(2,1)} %bitcast.4), calls=%async_computation | async-start | bytes 1310720 | tf_op jit(solution)/shard_map/all_to_all | solution.py:117
  22.1 22.1 %all-to-all-done = bf16[128,2,1280]{2,1,0:T(2,128)(2,1)S(1)} async-done(((bf16[128,2,1280]{2,1,0:T(2,128)(2,1)}), bf16[128,2,1280]{2,1,0:T(2,128)(2,1)S(1)}, u32[]{:S(2)}, u32[]{:S(2)}) %all-to-all-start) | async-done | bytes 655392 | tf_op jit(solution)/shard_map/all_to_all | solution.py:117
  44.3 0.1 reshape.110
  44.4 0.2 reshape.108
  44.6 0.3 convolution_convert_fusion
  44.9 0.0 copy-start.3
  45.0 0.0 copy-start.1
  45.0 1.1 %broadcast_in_dim.45 = bf16[4,8,16,1152]{3,2,1,0:T(8,128)(2,1)} broadcast(bf16[8,16,1152]{2,1,0:T(8,128)(2,1)S(1)} %bitcast.26), dimensions={1,2,3} | broadcast | bytes 1474560 | tf_op jit(solution)/shard_map/broadcast_in_dim | solution.py:137
  46.1 7.0 %all-to-all-start.1 = ((bf16[32,16,1152]{2,1,0:T(8,128)(2,1)}), bf16[32,16,1152]{2,1,0:T(8,128)(2,1)S(1)}, u32[]{:S(2)}, u32[]{:S(2)}) async-start(bf16[32,16,1152]{2,1,0:T(8,128)(2,1)} %bitcast.7), calls=%async_computation.1 | async-start | bytes 2359296 | tf_op jit(solution)/shard_map/all_to_all | solution.py:136
  53.0 0.0 copy-done.3
  53.1 0.7 broadcast_in_dim.49
  53.8 0.7 add.76
  54.5 0.8 add.77
  55.3 1.3 %add.71 = s32[2,2,32,8]{3,2,1,0:T(8,128)} broadcast(s32[2,8]{1,0:T(2,128)} %get-tuple-element.5), dimensions={0,3} | broadcast | bytes 4160 | tf_op jit(solution)/shard_map/add | solution.py:149
  56.6 0.9 %add.80 = s32[2,1,512]{2,1,0:T(1,128)S(1)} reshape(s32[2,2,32,8]{3,2,1,0:T(8,128)} %add.71) | data formatting | bytes 8192 | tf_op jit(solution)/shard_map/add | solution.py:149
  57.6 0.0 copy-done.1
  57.6 0.0 copy-start.2
  57.6 2.6 %copy.19 = bf16[128,16,576]{2,0,1:T(8,128)(2,1)} copy(bf16[128,16,576]{0,2,1:T(8,128)(2,1)S(1)} %copy-done.1) | data formatting | bytes 4718592 | tf_op args[0]
  60.2 0.0 copy-done.2
  60.2 0.6 add_select_fusion.place_ref
  60.8 10.4 %all-to-all-done.1.k_ref = bf16[32,16,1152]{2,1,0:T(8,128)(2,1)S(1)} async-done(((bf16[32,16,1152]{2,1,0:T(8,128)(2,1)}), bf16[32,16,1152]{2,1,0:T(8,128)(2,1)S(1)}, u32[]{:S(2)}, u32[]{:S(2)}) %all-to-all-start.1) | async-done | bytes 1179680 | tf_op jit(solution)/shard_map/all_to_all | solution.py:136
  71.2 0.0 copy-start
  71.2 1.0 %copy-done = bf16[32,16,1152]{2,1,0:T(8,128)(2,1)} copy-done((bf16[32,16,1152]{2,1,0:T(8,128)(2,1)}, bf16[32,16,1152]{2,1,0:T(8,128)(2,1)S(1)}, u32[]{:S(2)}) %copy-start) | copy-done | bytes 1179672
  72.2 7.3 %shard_map.46 = bf16[128,2048]{1,0:T(8,128)(2,1)} custom-call(s32[1]{0:T(128)} %bitcast.base_ref, bf16[16,128,576]{2,1,0:T(8,128)(2,1)} %bitcast.23, bf16[32,16,1152]{2,1,0:T(8,128)(2,1)} %copy-done, s32[2,1,512]{2,1,0:T(1,128)} %add_select_fusion.place_ref, bf16[16,512,128]{2,1,0:T(8,128)(2,1)} %w_ref.1), custom_call_target="tpu_custom_call" | custom-call | tf_op jit(solution)/shard_map/pallas_call | solution.py:68
  79.5 12.8 %all_to_all.29 = bf16[4,32,2048]{2,1,0:T(8,128)(2,1)S(1)} all-to-all(bf16[4,32,2048]{2,1,0:T(8,128)(2,1)} %bitcast.24), channel_id=1, replica_groups=mesh['ctx'=128,'head'=4] {'head'}, dimensions={0} | all-to-all | bytes 1048576 | tf_op jit(solution)/shard_map/all_to_all | solution.py:154
  92.4 0.8 copy.28
  (12 shorter events, 0.2 us)
Async XLA Ops:
  3.6 40.6 %all-to-all-start = ((bf16[128,2,1280]{2,1,0:T(2,128)(2,1)}), bf16[128,2,1280]{2,1,0:T(2,128)(2,1)S(1)}, u32[]{:S(2)}, u32[]{:S(2)}) async-start(bf16[128,2,1280]{2,1,0:T(2,128)(2,1)} %bitcast.4), calls=%async_computation | async-start | bytes 1310720 | tf_op jit(solution)/shard_map/all_to_all | solution.py:117
  44.9 8.1 %copy-start.3 = (s32[2,8]{1,0:T(2,128)S(1)}, s32[2,8]{1,0:T(2,128)}, u32[]{:S(2)}) copy-start(s32[2,8]{1,0:T(2,128)} %param.6) | copy-start | bytes 196
  45.0 12.6 %copy-start.1 = (bf16[128,16,576]{0,2,1:T(8,128)(2,1)S(1)}, bf16[128,16,576]{0,2,1:T(8,128)(2,1)}, u32[]{:S(2)}) copy-start(bf16[128,16,576]{0,2,1:T(8,128)(2,1)} %param.4) | copy-start | bytes 7077892
  46.1 25.1 %all-to-all-start.1 = ((bf16[32,16,1152]{2,1,0:T(8,128)(2,1)}), bf16[32,16,1152]{2,1,0:T(8,128)(2,1)S(1)}, u32[]{:S(2)}, u32[]{:S(2)}) async-start(bf16[32,16,1152]{2,1,0:T(8,128)(2,1)} %bitcast.7), calls=%async_computation.1 | async-start | bytes 2359296 | tf_op jit(solution)/shard_map/all_to_all | solution.py:136
  57.6 2.6 %copy-start.2 = (pred[2,1,512]{2,1,0:T(4,128)(4,1)S(1)}, pred[2,1,512]{2,1,0:T(4,128)(4,1)}, u32[]{:S(2)}) copy-start(pred[2,1,512]{2,1,0:T(4,128)(4,1)} %broadcast_in_dim.49) | copy-start | bytes 3076
  71.2 1.0 %copy-start = (bf16[32,16,1152]{2,1,0:T(8,128)(2,1)}, bf16[32,16,1152]{2,1,0:T(8,128)(2,1)S(1)}, u32[]{:S(2)}) copy-start(bf16[32,16,1152]{2,1,0:T(8,128)(2,1)S(1)} %all-to-all-done.1.k_ref) | copy-start | bytes 3538948

commit v3 on v2

v3 whole, which is shorter than its diff:
```python
import jax
import jax.numpy as jnp
from jax import lax
from jax.experimental import pallas as pl
from jax.experimental.pallas import tpu as pltpu
from jax.sharding import PartitionSpec as P

DC = 512
DR = 64
DV = 128
KBLK = 64
SEL = 8
WIDTH = DC + DR
BAND_TOKENS = 2
BAND = BAND_TOKENS * WIDTH
ROW = BAND + 128
Y, Z, CORES = 8, 8, 2
HEAD_BLOCK = 8
FACTOR = (DV + DR) ** -0.5 * 1.4426950408889634


def attend_kernel(base_ref, selected_ref, q_hbm, k_ref, w_ref, o_ref, keys_ref, q_ref, q_sems):
    heads, tokens, width = q_ref.shape
    bands, per_band, _ = k_ref.shape
    blocks = tokens // KBLK
    half = bands * SEL
    count = BAND_TOKENS * half

    copies = []
    for head in range(heads):
        copy = pltpu.make_async_copy(q_hbm.at[head], q_ref.at[head], q_sems.at[head])
        copy.start()
        copies.append(copy)

    lane = lax.broadcasted_iota(jnp.int32, (1, count), 1)
    slot = lane % SEL
    offset = (lane // SEL) % bands * BAND_TOKENS + lane // half
    biases = []
    for block in range(blocks):
        picked = slice(block * SEL, (block + 1) * SEL)
        for token in range(BAND_TOKENS):
            rows = k_ref[:, picked, token * width : (token + 1) * width]
            keys_ref[block, token * half : (token + 1) * half, :] = rows.reshape(half, width)
        chosen = jnp.full((1, count), -1, jnp.int32)
        for index in range(SEL):
            chosen = jnp.where(slot == index, selected_ref[block, index], chosen)
        place = jnp.where(chosen >= 0, chosen * KBLK + offset, 2**30)
        first = (base_ref[0] + block) * KBLK
        query_place = first + lax.broadcasted_iota(jnp.int32, (KBLK, 1), 0)
        biases.append(jnp.where(place <= query_place, 0.0, -1e30))

    def score(start, block):
        here = slice(block * KBLK, (block + 1) * KBLK)
        queries = q_ref[start : start + HEAD_BLOCK, here, :].reshape(HEAD_BLOCK * KBLK, width)
        return lax.dot_general(
            queries, keys_ref[block], (((1,), (1,)), ((), ())), preferred_element_type=jnp.float32
        )

    def finish(start, block, scores):
        here = slice(block * KBLK, (block + 1) * KBLK)
        scores = scores.reshape(HEAD_BLOCK, KBLK, count) * FACTOR + biases[block][None]
        powered = jnp.exp2(scores - jnp.max(scores, axis=2, keepdims=True))
        total = jnp.sum(powered, axis=2, keepdims=True)
        mixed = lax.dot_general(
            powered.astype(jnp.bfloat16).reshape(HEAD_BLOCK * KBLK, count),
            keys_ref[block][:, :DC],
            (((1,), (0,)), ((), ())),
            preferred_element_type=jnp.float32,
        ).astype(jnp.bfloat16)
        for head in range(HEAD_BLOCK):
            columns = slice((start + head) * DV, (start + head + 1) * DV)
            expanded = jnp.dot(
                mixed[head * KBLK : (head + 1) * KBLK],
                w_ref[start + head],
                preferred_element_type=jnp.float32,
            )
            o_ref[here, columns] = (expanded / total[head]).astype(jnp.bfloat16)

    chunks = [(start, block) for start in range(0, heads, HEAD_BLOCK) for block in range(blocks)]
    waiting = None
    for start, block in chunks:
        if block == 0:
            for copy in copies[start : start + HEAD_BLOCK]:
                copy.wait()
        scores = score(start, block)
        if waiting is not None:
            finish(*waiting)
        waiting = (start, block, scores)
    finish(*waiting)


def attend(base, selected, queries, keys, value_weight):
    heads, tokens, width = queries.shape
    blocks = selected.shape[0]
    vmem = pl.BlockSpec(memory_space=pltpu.VMEM)
    smem = pl.BlockSpec(memory_space=pltpu.SMEM)
    return pl.pallas_call(
        attend_kernel,
        out_shape=jax.ShapeDtypeStruct((tokens, heads * DV), jnp.bfloat16),
        in_specs=[smem, smem, pl.BlockSpec(memory_space=pltpu.HBM), vmem, vmem],
        out_specs=vmem,
        scratch_shapes=[
            pltpu.VMEM((blocks, SEL * KBLK, width), jnp.bfloat16),
            pltpu.VMEM(queries.shape, queries.dtype),
            pltpu.SemaphoreType.DMA((heads,)),
        ],
        compiler_params=pltpu.CompilerParams(vmem_limit_bytes=32 * 2**20),
    )(base, selected, pltpu.with_memory_space_constraint(queries, pltpu.HBM), keys, value_weight)


def spread_kernel(head_ref, selected_ref, latent_ref, out_ref, band_ref, in_sem, out_sem):
    cell, here, row = band_ref.shape
    first = head_ref[0] * (cell * BAND)
    incoming = []
    for place in range(cell):
        columns = pl.ds(pl.multiple_of(first + place * BAND, 128), BAND)
        copy = pltpu.make_async_copy(
            latent_ref.at[:, columns], band_ref.at[place, :, pl.ds(0, BAND)], in_sem.at[place]
        )
        copy.start()
        incoming.append(copy)
    lists = selected_ref[...].astype(jnp.bfloat16)
    for place in range(cell):
        band_ref[place, :, BAND:] = jnp.zeros((here, row - BAND), jnp.bfloat16)
        band_ref[place, :, BAND : BAND + SEL] = lists
    for copy in incoming:
        copy.wait()
    outgoing = []
    for y in range(Y // 2):
        for z in range(Z // 2):
            for dy in range(2):
                half = pl.ds(dy * cell // 2, cell // 2)
                copy = pltpu.make_async_copy(
                    band_ref.at[half], out_ref.at[y, dy, z], out_sem.at[len(outgoing)]
                )
                copy.start()
                outgoing.append(copy)
    for copy in outgoing:
        copy.wait()


def spread_bands(head, selected, latent_cache):
    here = selected.shape[0]
    cell = 4 * CORES
    hbm = pl.BlockSpec(memory_space=pltpu.HBM)
    return pl.pallas_call(
        spread_kernel,
        out_shape=jax.ShapeDtypeStruct((Y // 2, 2, Z // 2, cell // 2, here, ROW), jnp.bfloat16),
        in_specs=[
            pl.BlockSpec(memory_space=pltpu.SMEM),
            pl.BlockSpec(memory_space=pltpu.VMEM),
            hbm,
        ],
        out_specs=hbm,
        scratch_shapes=[
            pltpu.VMEM((cell, here, ROW), jnp.bfloat16),
            pltpu.SemaphoreType.DMA((cell,)),
            pltpu.SemaphoreType.DMA((Y * Z // 2,)),
        ],
    )(head.astype(jnp.int32).reshape(1), selected, latent_cache)


def stage_kernel(raw_hbm, w_hbm, q_hbm, w_ref, raw_ref, q_ref, sems, out_sems):
    heads, tokens, _ = q_ref.shape
    w_copy = pltpu.make_async_copy(w_hbm, w_ref, sems.at[heads])
    w_copy.start()
    copies = []
    for head in range(heads):
        copy = pltpu.make_async_copy(raw_hbm.at[head], raw_ref.at[head], sems.at[head])
        copy.start()
        copies.append(copy)
    same = lax.broadcasted_iota(jnp.int32, (tokens, tokens), 0) == lax.broadcasted_iota(
        jnp.int32, (tokens, tokens), 1
    )
    unit = same.astype(jnp.float32).astype(jnp.bfloat16)
    for head in range(heads):
        copies[head].wait()
        turned = lax.dot_general(
            unit, raw_ref[head], (((1,), (1,)), ((), ())), preferred_element_type=jnp.float32
        )
        q_ref[head] = turned.astype(jnp.bfloat16)
    for head in range(heads):
        copies[head] = pltpu.make_async_copy(q_ref.at[head], q_hbm.at[head], out_sems.at[head])
        copies[head].start()
    for copy in copies:
        copy.wait()
    w_copy.wait()


def stage(queries, value_weight):
    tokens, heads, width = queries.shape
    hbm = pl.BlockSpec(memory_space=pltpu.HBM)
    vmem = pl.BlockSpec(memory_space=pltpu.VMEM)
    raw = queries.transpose(1, 2, 0)
    return pl.pallas_call(
        stage_kernel,
        out_shape=(
            jax.ShapeDtypeStruct((heads, tokens, width), queries.dtype),
            jax.ShapeDtypeStruct(value_weight.shape, value_weight.dtype),
        ),
        in_specs=[hbm, hbm],
        out_specs=(hbm, vmem),
        scratch_shapes=[
            pltpu.VMEM((heads, width, tokens), queries.dtype),
            pltpu.VMEM((heads, tokens, width), queries.dtype),
            pltpu.SemaphoreType.DMA((heads + 1,)),
            pltpu.SemaphoreType.DMA((heads,)),
        ],
        compiler_params=pltpu.CompilerParams(vmem_limit_bytes=16 * 2**20),
        cost_estimate=pl.CostEstimate(flops=10**9, transcendentals=0, bytes_accessed=10 * 2**20),
    )(
        pltpu.with_memory_space_constraint(raw, pltpu.HBM),
        pltpu.with_memory_space_constraint(value_weight, pltpu.HBM),
    )


def fetch_groups(heads):
    groups = []
    for y in range(Y // 2):
        for z in range(Z // 2):
            groups.append([
                (((2 * y + dy) * Z + 2 * z + dz) * CORES + core) * heads + head
                for head in range(heads)
                for dy in range(2)
                for dz in range(2)
                for core in range(CORES)
            ])
    return groups


def per_device(queries, latent_cache, selected, value_weight):
    ctx_size = lax.axis_size("ctx")
    heads = lax.axis_size("head")
    ctx = lax.axis_index("ctx")
    head = lax.axis_index("head")
    here = selected.shape[0]
    cell = 4 * CORES
    bands = heads * cell

    spread = lax.all_to_all(
        spread_bands(head, selected, latent_cache).reshape(ctx_size, here, ROW),
        "ctx",
        split_axis=0,
        concat_axis=0,
        tiled=True,
    )
    table = spread.reshape(ctx_size * here, ROW)

    lists = spread[:, :, BAND : BAND + SEL].reshape(Y // 2, 2, Z // 2, 2, CORES, here, SEL)
    y, z = ctx // (Z * CORES), (ctx // CORES) % Z
    lists = lax.dynamic_slice_in_dim(lists, y // 2, 1, 0)
    lists = lax.dynamic_slice_in_dim(lists, z // 2, 1, 2)
    wanted = lists.astype(jnp.int32).reshape(-1)
    chosen = wanted[:, None] == jnp.arange(ctx_size * here, dtype=jnp.int32)[None, :]
    picked = jnp.dot(
        chosen.astype(jnp.bfloat16), table[:, :BAND], preferred_element_type=jnp.float32
    ).astype(jnp.bfloat16)
    picked = picked.reshape(1, cell, here * SEL, BAND)
    keys = lax.all_to_all(
        jnp.broadcast_to(picked, (heads, cell, here * SEL, BAND)).reshape(bands, here * SEL, BAND),
        ("ctx", "head"),
        split_axis=0,
        concat_axis=0,
        axis_index_groups=fetch_groups(heads),
        tiled=True,
    )

    base = (ctx * here).astype(jnp.int32).reshape(1)
    turned, mapping = stage(queries, value_weight)
    attended = attend(base, selected, turned, keys, mapping)
    return lax.all_to_all(attended, "head", split_axis=0, concat_axis=1, tiled=True)


def solution(mesh):
    in_specs = (P("ctx", "head", None), P("ctx", None), P("ctx", None), P("head", None, None))
    out_specs = P(("ctx", "head"), None)
    return jax.shard_map(
        per_device, mesh=mesh, in_specs=in_specs, out_specs=out_specs, check_vma=False
    )
```

time: 93.7 us -> 89.2 us (0.952)
  Pallas kernels: 7.3 us -> 17.4 us
  local copies, waits for them, and re-layouts: 12.7 us -> 3.88 us
  waiting for transfers between devices: 32.5 us -> 30.1 us
  other arithmetic: 1.96 us -> 0.02 us
  blocking collectives: 12.8 us -> 11.8 us
    pallas_call x0 -> x2, Pallas kernels: none -> 11.3 us  [the longest x1 8.6 us: stage(): pl.pallas_call(stage_kernel, out_shape=(jax.ShapeDtypeStruct((heads, toke...]
    add x4 -> x0, local copies, waits for them, and re-layouts: 3.77 us -> none  [per_device(): place = selected[:, None, None, :] * KBLK + offsets[None, :, :, None]]
    unnamed x11 -> x5, local copies, waits for them, and re-layouts: 4.56 us -> 1.53 us
    all_to_all x1, waiting for transfers between devices: 10.4 us -> 7.99 us  [per_device(): lax.all_to_all(jnp.broadcast_to(picked, (heads, cell, here * SEL, BAND))....]
    broadcast_in_dim x6 -> x0, local copies, waits for them, and re-layouts: 1.92 us -> none  [the longest x2 1.21 us: per_device(): jnp.broadcast_to(mine, (Y // 2, 2, Z // 2, 2, CORES, here, ROW))]
    mul x2 -> x0, other arithmetic: 1.33 us -> none  [the longest x1 1.33 us: per_device(): place = selected[:, None, None, :] * KBLK + offsets[None, :, :, None]]
    pallas_call x1, Pallas kernels: 7.3 us -> 6.08 us  [attend(): pl.pallas_call(attend_kernel, out_shape=jax.ShapeDtypeStruct((tokens, hea...]
    all_to_all x1, blocking collectives: 12.8 us -> 11.8 us  [per_device(): lax.all_to_all(attended, 'head', split_axis=0, concat_axis=1, tiled=True)]
  transfers between devices with their start and end apart: 2 -> 2, of which waited for: 2 -> 2; matrix products, arithmetic and copies ran while one was open for 8% -> 0% of each run, Pallas kernels for 0% -> 10%
where the time goes in v3:
time: 89.2 us; the launch traced here: 88.9 us
  waiting for transfers between devices  30.1 us (34%)
  starting transfers between devices  25.2 us (28%)
  Pallas kernels  17.4 us (20%)
  blocking collectives  11.8 us (13%)
  local copies, waits for them, and re-layouts  3.88 us (4%)
    all_to_all x1, waiting for transfers between devices, per_device(): lax.all_to_all(spread_bands(head, selected, latent_cache).reshape(ctx_siz...  22.1 us
    all_to_all x1, starting transfers between devices, per_device(): lax.all_to_all(spread_bands(head, selected, latent_cache).reshape(ctx_siz...  18.4 us
    all_to_all x1, blocking collectives, per_device(): lax.all_to_all(attended, 'head', split_axis=0, concat_axis=1, tiled=True)  11.8 us
    pallas_call x1, Pallas kernels, stage(): pl.pallas_call(stage_kernel, out_shape=(jax.ShapeDtypeStruct((heads, toke...  8.6 us
    all_to_all x1, waiting for transfers between devices, per_device(): lax.all_to_all(jnp.broadcast_to(picked, (heads, cell, here * SEL, BAND))....  7.99 us
    all_to_all x1, starting transfers between devices, per_device(): lax.all_to_all(jnp.broadcast_to(picked, (heads, cell, here * SEL, BAND))....  6.82 us
    pallas_call x1, Pallas kernels, attend(): pl.pallas_call(attend_kernel, out_shape=jax.ShapeDtypeStruct((tokens, hea...  6.08 us
    pallas_call x1, Pallas kernels, spread_bands(): pl.pallas_call(spread_kernel, out_shape=jax.ShapeDtypeStruct((Y // 2, 2,...  2.67 us
  transfers between devices with their start and end apart: 2, of which 2 were waited for; matrix products, arithmetic and copies ran while one was open for 0% of the time, Pallas kernels for 10%

profile of v3, /device:TPU:1, one launch (start us, length us, event | category | flops | bytes accessed | tf_op | source)
XLA Modules:
  0.0 88.9 jit_solution(14818958246892916128)
XLA Ops:
  0.0 2.7 %shard_map.47 = bf16[4,2,4,4,2,1280]{5,4,3,2,1,0:T(2,128)(2,1)} custom-call(s32[1]{0:T(128)} %bitcast.2.head_ref, s32[2,8]{1,0:T(2,128)} %selected_ref.3, bf16[2,36864]{1,0:T(2,128)(2,1)} %latent_ref.1), custom_call_target="tpu_custom_call" | custom-call | tf_op jit(solution)/shard_map/pallas_call | solution.py:146
  2.7 18.4 %all-to-all-start = ((bf16[128,2,1280]{2,1,0:T(2,128)(2,1)}), bf16[128,2,1280]{2,1,0:T(2,128)(2,1)S(1)}, u32[]{:S(2)}, u32[]{:S(2)}) async-start(bf16[128,2,1280]{2,1,0:T(2,128)(2,1)} %bitcast.14), calls=%async_computation | async-start | bytes 1310720 | tf_op jit(solution)/shard_map/all_to_all | solution.py:240
  21.2 22.1 %all-to-all-done = bf16[128,2,1280]{2,1,0:T(2,128)(2,1)S(1)} async-done(((bf16[128,2,1280]{2,1,0:T(2,128)(2,1)}), bf16[128,2,1280]{2,1,0:T(2,128)(2,1)S(1)}, u32[]{:S(2)}, u32[]{:S(2)}) %all-to-all-start) | async-done | bytes 655392 | tf_op jit(solution)/shard_map/all_to_all | solution.py:240
  43.4 0.1 reshape.30
  43.5 0.2 reshape.28
  43.7 0.3 convolution_convert_fusion
  44.0 1.1 %broadcast_in_dim.9 = bf16[4,8,16,1152]{3,2,1,0:T(8,128)(2,1)} broadcast(bf16[8,16,1152]{2,1,0:T(8,128)(2,1)S(1)} %bitcast.17), dimensions={1,2,3} | broadcast | bytes 1474560 | tf_op jit(solution)/shard_map/broadcast_in_dim | solution.py:260
  45.2 6.8 %all-to-all-start.1 = ((bf16[32,16,1152]{2,1,0:T(8,128)(2,1)}), bf16[32,16,1152]{2,1,0:T(8,128)(2,1)S(1)}, u32[]{:S(2)}, u32[]{:S(2)}) async-start(bf16[32,16,1152]{2,1,0:T(8,128)(2,1)} %bitcast.6), calls=%async_computation.1 | async-start | bytes 2359296 | tf_op jit(solution)/shard_map/all_to_all | solution.py:259
  52.0 0.0 copy-start.1
  52.0 8.6 %shard_map.46 = (bf16[16,128,576]{2,1,0:T(8,128)(2,1)S(1)}, bf16[16,512,128]{2,1,0:T(8,128)(2,1)S(1)}) custom-call(bf16[16,576,128]{2,1,0:T(8,128)(2,1)} %bitcast.15, bf16[16,512,128]{2,1,0:T(8,128)(2,1)} %w_hbm.1), custom_call_target="tpu_custom_call" | custom-call | flops 1000000000 | bytes 10485760 | tf_op jit(solution)/shard_map/pallas_call | solution.py:195
  60.6 0.0 copy-start
  60.6 1.5 %copy-done = bf16[16,128,576]{2,1,0:T(8,128)(2,1)} copy-done((bf16[16,128,576]{2,1,0:T(8,128)(2,1)}, bf16[16,128,576]{2,1,0:T(8,128)(2,1)S(1)}, u32[]{:S(2)}) %copy-start) | copy-done | bytes 2359320
  62.1 8.0 %all-to-all-done.1.k_ref = bf16[32,16,1152]{2,1,0:T(8,128)(2,1)S(1)} async-done(((bf16[32,16,1152]{2,1,0:T(8,128)(2,1)}), bf16[32,16,1152]{2,1,0:T(8,128)(2,1)S(1)}, u32[]{:S(2)}, u32[]{:S(2)}) %all-to-all-start.1) | async-done | bytes 1179680 | tf_op jit(solution)/shard_map/all_to_all | solution.py:259
  70.1 0.0 copy-done.1
  70.1 6.1 %shard_map.48 = bf16[128,2048]{1,0:T(8,128)(2,1)S(1)} custom-call(s32[1]{0:T(128)} %bitcast.base_ref, s32[2,8]{1,0:T(2,128)S(1)} %copy-done.1, bf16[16,128,576]{2,1,0:T(8,128)(2,1)} %copy-done, bf16[32,16,1152]{2,1,0:T(8,128)(2,1)S(1)} %all-to-all-done.1.k_ref, bf16[16,512,128]{2,1,0:T(8,128)(2,1)S(1)} %get-tuple-element.8.w_ref), custom_call_target="tpu_custom_call" | custom-call | tf_op jit(solution)/shard_map/pallas_call | solution.py:97
  76.2 11.8 %all_to_all.29 = bf16[4,32,2048]{2,1,0:T(8,128)(2,1)S(1)} all-to-all(bf16[4,32,2048]{2,1,0:T(8,128)(2,1)S(1)} %bitcast.13), channel_id=1, replica_groups=mesh['ctx'=128,'head'=4] {'head'}, dimensions={0} | all-to-all | bytes 1048576 | tf_op jit(solution)/shard_map/all_to_all | solution.py:271
  88.0 0.8 copy.17
  (4 shorter events, 0.1 us)
Async XLA Ops:
  2.7 40.6 %all-to-all-start = ((bf16[128,2,1280]{2,1,0:T(2,128)(2,1)}), bf16[128,2,1280]{2,1,0:T(2,128)(2,1)S(1)}, u32[]{:S(2)}, u32[]{:S(2)}) async-start(bf16[128,2,1280]{2,1,0:T(2,128)(2,1)} %bitcast.14), calls=%async_computation | async-start | bytes 1310720 | tf_op jit(solution)/shard_map/all_to_all | solution.py:240
  45.2 25.0 %all-to-all-start.1 = ((bf16[32,16,1152]{2,1,0:T(8,128)(2,1)}), bf16[32,16,1152]{2,1,0:T(8,128)(2,1)S(1)}, u32[]{:S(2)}, u32[]{:S(2)}) async-start(bf16[32,16,1152]{2,1,0:T(8,128)(2,1)} %bitcast.6), calls=%async_computation.1 | async-start | bytes 2359296 | tf_op jit(solution)/shard_map/all_to_all | solution.py:259
  52.0 18.1 %copy-start.1 = (s32[2,8]{1,0:T(2,128)S(1)}, s32[2,8]{1,0:T(2,128)}, u32[]{:S(2)}) copy-start(s32[2,8]{1,0:T(2,128)} %selected_ref.3) | copy-start | bytes 196
  60.6 1.5 %copy-start = (bf16[16,128,576]{2,1,0:T(8,128)(2,1)}, bf16[16,128,576]{2,1,0:T(8,128)(2,1)S(1)}, u32[]{:S(2)}) copy-start(bf16[16,128,576]{2,1,0:T(8,128)(2,1)S(1)} %get-tuple-element.7.q_hbm) | copy-start | bytes 7077892

commit v4 on v3

v4 whole, which is shorter than its diff:
```python
import jax
import jax.numpy as jnp
from jax import lax
from jax.experimental import pallas as pl
from jax.experimental.pallas import tpu as pltpu
from jax.sharding import PartitionSpec as P

DC = 512
DR = 64
DV = 128
KBLK = 64
SEL = 8
WIDTH = DC + DR
BAND_TOKENS = 2
BAND = BAND_TOKENS * WIDTH
ROW = BAND + 128
Y, Z, CORES = 8, 8, 2
FACTOR = (DV + DR) ** -0.5 * 1.4426950408889634


def attend_kernel(low_ref, high_hbm, k_ref, place_ref, w_hbm, o_ref, keys_ref, high_ref, w_ref, sems):
    part, tokens, width = low_ref.shape
    heads = w_ref.shape[0]
    bands, per_band, _ = k_ref.shape
    blocks = tokens // KBLK
    half = bands * SEL
    count = BAND_TOKENS * half

    low, high = pl.ds(0, part), pl.ds(part, part)
    copies = [
        pltpu.make_async_copy(w_hbm.at[low], w_ref.at[low], sems.at[0]),
        pltpu.make_async_copy(high_hbm, high_ref, sems.at[1]),
        pltpu.make_async_copy(w_hbm.at[high], w_ref.at[high], sems.at[2]),
    ]
    for copy in copies:
        copy.start()

    biases = []
    for block in range(blocks):
        picked = slice(block * SEL, (block + 1) * SEL)
        for token in range(BAND_TOKENS):
            rows = k_ref[:, picked, token * width : (token + 1) * width]
            keys_ref[block, token * half : (token + 1) * half, :] = rows.reshape(half, width)
        query_place = lax.broadcasted_iota(jnp.int32, (KBLK, 1), 0)
        biases.append(jnp.where(place_ref[block] <= query_place, 0.0, -1e30))

    def score(group, block):
        here = slice(block * KBLK, (block + 1) * KBLK)
        queries = (high_ref if group else low_ref)[:, here, :].reshape(part * KBLK, width)
        return lax.dot_general(
            queries, keys_ref[block], (((1,), (1,)), ((), ())), preferred_element_type=jnp.float32
        )

    def finish(group, block, scores):
        here = slice(block * KBLK, (block + 1) * KBLK)
        scores = scores.reshape(part, KBLK, count) * FACTOR + biases[block][None]
        powered = jnp.exp2(scores - jnp.max(scores, axis=2, keepdims=True))
        total = jnp.sum(powered, axis=2, keepdims=True)
        mixed = lax.dot_general(
            powered.astype(jnp.bfloat16).reshape(part * KBLK, count),
            keys_ref[block][:, :DC],
            (((1,), (0,)), ((), ())),
            preferred_element_type=jnp.float32,
        ).astype(jnp.bfloat16)
        if block == 0:
            copies[2 if group else 0].wait()
        for index in range(part):
            head = group * part + index
            columns = slice(head * DV, (head + 1) * DV)
            expanded = jnp.dot(
                mixed[index * KBLK : (index + 1) * KBLK],
                w_ref[head],
                preferred_element_type=jnp.float32,
            )
            o_ref[here, columns] = (expanded / total[index]).astype(jnp.bfloat16)

    waiting = None
    for group in range(heads // part):
        for block in range(blocks):
            if group and block == 0:
                copies[1].wait()
            scores = score(group, block)
            if waiting is not None:
                finish(*waiting)
            waiting = (group, block, scores)
    finish(*waiting)


def attend(low, high, keys, place, value_weight):
    part, tokens, width = low.shape
    heads = value_weight.shape[0]
    blocks = tokens // KBLK
    vmem = pl.BlockSpec(memory_space=pltpu.VMEM)
    hbm = pl.BlockSpec(memory_space=pltpu.HBM)
    return pl.pallas_call(
        attend_kernel,
        out_shape=jax.ShapeDtypeStruct((tokens, heads * DV), jnp.bfloat16),
        in_specs=[vmem, hbm, vmem, vmem, hbm],
        out_specs=vmem,
        scratch_shapes=[
            pltpu.VMEM((blocks, SEL * KBLK, width), jnp.bfloat16),
            pltpu.VMEM(high.shape, high.dtype),
            pltpu.VMEM(value_weight.shape, value_weight.dtype),
            pltpu.SemaphoreType.DMA((3,)),
        ],
        compiler_params=pltpu.CompilerParams(vmem_limit_bytes=32 * 2**20),
    )(
        low,
        pltpu.with_memory_space_constraint(high, pltpu.HBM),
        keys,
        place,
        pltpu.with_memory_space_constraint(value_weight, pltpu.HBM),
    )


def spread_kernel(selected_hbm, latent_hbm, out_hbm, band_ref, selected_ref, in_sem, out_sem):
    cell, here, row = band_ref.shape
    first = lax.axis_index("head") * (cell * BAND)
    incoming = [pltpu.make_async_copy(selected_hbm, selected_ref, in_sem.at[cell])]
    for place in range(cell):
        columns = pl.ds(pl.multiple_of(first + place * BAND, 128), BAND)
        incoming.append(
            pltpu.make_async_copy(
                latent_hbm.at[:, columns], band_ref.at[place, :, pl.ds(0, BAND)], in_sem.at[place]
            )
        )
    for copy in incoming:
        copy.start()
    for place in range(cell):
        band_ref[place, :, BAND:] = jnp.zeros((here, row - BAND), jnp.bfloat16)
    incoming[0].wait()
    lists = selected_ref[...].astype(jnp.bfloat16)
    for place in range(cell):
        band_ref[place, :, BAND : BAND + SEL] = lists
    for copy in incoming[1:]:
        copy.wait()
    outgoing = []
    for y in range(Y // 2):
        for z in range(Z // 2):
            for dy in range(2):
                half = pl.ds(dy * cell // 2, cell // 2)
                copy = pltpu.make_async_copy(
                    band_ref.at[half], out_hbm.at[y, dy, z], out_sem.at[len(outgoing)]
                )
                copy.start()
                outgoing.append(copy)
    for copy in outgoing:
        copy.wait()


def spread_bands(selected, latent_cache):
    here = selected.shape[0]
    cell = 4 * CORES
    hbm = pl.BlockSpec(memory_space=pltpu.HBM)
    return pl.pallas_call(
        spread_kernel,
        out_shape=jax.ShapeDtypeStruct((Y // 2, 2, Z // 2, cell // 2, here, ROW), jnp.bfloat16),
        in_specs=[hbm, hbm],
        out_specs=hbm,
        scratch_shapes=[
            pltpu.VMEM((cell, here, ROW), jnp.bfloat16),
            pltpu.VMEM(selected.shape, jnp.int32),
            pltpu.SemaphoreType.DMA((cell + 1,)),
            pltpu.SemaphoreType.DMA((Y * Z // 2,)),
        ],
    )(
        pltpu.with_memory_space_constraint(selected, pltpu.HBM),
        pltpu.with_memory_space_constraint(latent_cache, pltpu.HBM),
    )


def stage_kernel(selected_ref, raw_hbm, low_ref, high_hbm, place_ref, raw_ref, high_ref, sems, out_sem):
    heads, _, tokens = raw_ref.shape
    part = low_ref.shape[0]
    copies = []
    for head in range(heads):
        copy = pltpu.make_async_copy(raw_hbm.at[head], raw_ref.at[head], sems.at[head])
        copy.start()
        copies.append(copy)

    blocks, _, count = place_ref.shape
    lane = lax.broadcasted_iota(jnp.int32, (1, count), 1)
    slot = lane % SEL
    half = count // BAND_TOKENS
    offset = (lane % half) // SEL * BAND_TOKENS + lane // half
    for block in range(blocks):
        chosen = jnp.full((1, count), -1, jnp.int32)
        for index in range(SEL):
            chosen = jnp.where(slot == index, selected_ref[block, index], chosen)
        own = lax.axis_index("ctx") * blocks + block
        place_ref[block] = jnp.where(chosen >= 0, (chosen - own) * KBLK + offset, 2**30)

    same = lax.broadcasted_iota(jnp.int32, (tokens, tokens), 0) == lax.broadcasted_iota(
        jnp.int32, (tokens, tokens), 1
    )
    unit = same.astype(jnp.float32).astype(jnp.bfloat16)
    for head in range(heads):
        copies[head].wait()
        turned = lax.dot_general(
            unit, raw_ref[head], (((1,), (1,)), ((), ())), preferred_element_type=jnp.float32
        ).astype(jnp.bfloat16)
        if head < part:
            low_ref[head] = turned
        else:
            high_ref[head - part] = turned
    copy = pltpu.make_async_copy(high_ref, high_hbm, out_sem)
    copy.start()
    copy.wait()


def stage(selected, queries):
    tokens, heads, width = queries.shape
    blocks = selected.shape[0]
    hbm = pl.BlockSpec(memory_space=pltpu.HBM)
    vmem = pl.BlockSpec(memory_space=pltpu.VMEM)
    group = jax.ShapeDtypeStruct((heads // 2, tokens, width), queries.dtype)
    return pl.pallas_call(
        stage_kernel,
        out_shape=(group, group, jax.ShapeDtypeStruct((blocks, 1, SEL * KBLK), jnp.int32)),
        in_specs=[pl.BlockSpec(memory_space=pltpu.SMEM), hbm],
        out_specs=(vmem, hbm, vmem),
        scratch_shapes=[
            pltpu.VMEM((heads, width, tokens), queries.dtype),
            pltpu.VMEM(group.shape, queries.dtype),
            pltpu.SemaphoreType.DMA((heads,)),
            pltpu.SemaphoreType.DMA,
        ],
        compiler_params=pltpu.CompilerParams(vmem_limit_bytes=16 * 2**20),
        cost_estimate=pl.CostEstimate(flops=10**9, transcendentals=0, bytes_accessed=10 * 2**20),
    )(selected, pltpu.with_memory_space_constraint(queries.transpose(1, 2, 0), pltpu.HBM))


def fetch_groups(heads):
    groups = []
    for y in range(Y // 2):
        for z in range(Z // 2):
            groups.append([
                (((2 * y + dy) * Z + 2 * z + dz) * CORES + core) * heads + head
                for head in range(heads)
                for dy in range(2)
                for dz in range(2)
                for core in range(CORES)
            ])
    return groups


def per_device(queries, latent_cache, selected, value_weight):
    ctx_size = lax.axis_size("ctx")
    heads = lax.axis_size("head")
    ctx = lax.axis_index("ctx")
    here = selected.shape[0]
    cell = 4 * CORES
    bands = heads * cell

    spread = lax.all_to_all(
        spread_bands(selected, latent_cache).reshape(ctx_size, here, ROW),
        "ctx",
        split_axis=0,
        concat_axis=0,
        tiled=True,
    )
    table = spread.reshape(ctx_size * here, ROW)

    lists = spread[:, :, BAND : BAND + SEL].reshape(Y // 2, 2, Z // 2, 2, CORES, here, SEL)
    y, z = ctx // (Z * CORES), (ctx // CORES) % Z
    lists = lax.dynamic_slice_in_dim(lists, y // 2, 1, 0)
    lists = lax.dynamic_slice_in_dim(lists, z // 2, 1, 2)
    wanted = lists.astype(jnp.int32).reshape(-1)
    chosen = wanted[:, None] == jnp.arange(ctx_size * here, dtype=jnp.int32)[None, :]
    picked = jnp.dot(
        chosen.astype(jnp.bfloat16), table[:, :BAND], preferred_element_type=jnp.float32
    ).astype(jnp.bfloat16)
    picked = picked.reshape(1, cell, here * SEL, BAND)
    keys = lax.all_to_all(
        jnp.broadcast_to(picked, (heads, cell, here * SEL, BAND)).reshape(bands, here * SEL, BAND),
        ("ctx", "head"),
        split_axis=0,
        concat_axis=0,
        axis_index_groups=fetch_groups(heads),
        tiled=True,
    )

    low, high, place = stage(selected, queries)
    attended = attend(low, high, keys, place, value_weight)
    return lax.all_to_all(attended, "head", split_axis=0, concat_axis=1, tiled=True)


def solution(mesh):
    in_specs = (P("ctx", "head", None), P("ctx", None), P("ctx", None), P("head", None, None))
    out_specs = P(("ctx", "head"), None)
    return jax.shard_map(
        per_device, mesh=mesh, in_specs=in_specs, out_specs=out_specs, check_vma=False
    )
```

time: 89.2 us -> 87.9 us (0.985)
  Pallas kernels: 17.4 us -> 12.4 us
  waiting for transfers between devices: 30.1 us -> 34 us
    all_to_all x1, waiting for transfers between devices: 7.99 us -> 12 us  [per_device(): lax.all_to_all(jnp.broadcast_to(picked, (heads, cell, here * SEL, BAND))....]
    pallas_call x1, Pallas kernels: 8.6 us -> 5.08 us  [stage(): pl.pallas_call(stage_kernel, out_shape=(group, group, jax.ShapeDtypeStruc...]
  transfers between devices with their start and end apart: 2 -> 2, of which waited for: 2 -> 2; matrix products, arithmetic and copies ran while one was open for 0% -> 0% of each run, Pallas kernels for 10% -> 6%
where the time goes in v4:
time: 87.9 us; the launch traced here: 87.6 us
  waiting for transfers between devices  34 us (39%)
  starting transfers between devices  25.4 us (29%)
  Pallas kernels  12.4 us (14%)
  blocking collectives  11.8 us (13%)
  local copies, waits for them, and re-layouts  3.41 us (4%)
    all_to_all x1, waiting for transfers between devices, per_device(): lax.all_to_all(spread_bands(selected, latent_cache).reshape(ctx_size, her...  22.1 us
    all_to_all x1, starting transfers between devices, per_device(): lax.all_to_all(spread_bands(selected, latent_cache).reshape(ctx_size, her...  18.4 us
    all_to_all x1, waiting for transfers between devices, per_device(): lax.all_to_all(jnp.broadcast_to(picked, (heads, cell, here * SEL, BAND))....  12 us
    all_to_all x1, blocking collectives, per_device(): lax.all_to_all(attended, 'head', split_axis=0, concat_axis=1, tiled=True)  11.8 us
    all_to_all x1, starting transfers between devices, per_device(): lax.all_to_all(jnp.broadcast_to(picked, (heads, cell, here * SEL, BAND))....  6.96 us
    pallas_call x1, Pallas kernels, attend(): pl.pallas_call(attend_kernel, out_shape=jax.ShapeDtypeStruct((tokens, hea...  5.32 us
    pallas_call x1, Pallas kernels, stage(): pl.pallas_call(stage_kernel, out_shape=(group, group, jax.ShapeDtypeStruc...  5.08 us
    pallas_call x1, Pallas kernels, spread_bands(): pl.pallas_call(spread_kernel, out_shape=jax.ShapeDtypeStruct((Y // 2, 2,...  2.02 us
  transfers between devices with their start and end apart: 2, of which 2 were waited for; matrix products, arithmetic and copies ran while one was open for 0% of the time, Pallas kernels for 6%

profile of v4, /device:TPU:1, one launch (start us, length us, event | category | flops | bytes accessed | tf_op | source)
XLA Modules:
  0.0 87.6 jit_solution(16080685275893575697)
XLA Ops:
  0.0 2.0 %shard_map.47 = bf16[4,2,4,4,2,1280]{5,4,3,2,1,0:T(2,128)(2,1)} custom-call(s32[2,8]{1,0:T(2,128)} %selected_hbm.1, bf16[2,36864]{1,0:T(2,128)(2,1)} %latent_hbm.1), custom_call_target="tpu_custom_call" | custom-call | tf_op jit(solution)/shard_map/pallas_call | solution.py:155
  2.0 18.4 %all-to-all-start = ((bf16[128,2,1280]{2,1,0:T(2,128)(2,1)}), bf16[128,2,1280]{2,1,0:T(2,128)(2,1)S(1)}, u32[]{:S(2)}, u32[]{:S(2)}) async-start(bf16[128,2,1280]{2,1,0:T(2,128)(2,1)} %bitcast.12), calls=%async_computation | async-start | bytes 1310720 | tf_op jit(solution)/shard_map/all_to_all | solution.py:255
  20.5 22.1 %all-to-all-done = bf16[128,2,1280]{2,1,0:T(2,128)(2,1)S(1)} async-done(((bf16[128,2,1280]{2,1,0:T(2,128)(2,1)}), bf16[128,2,1280]{2,1,0:T(2,128)(2,1)S(1)}, u32[]{:S(2)}, u32[]{:S(2)}) %all-to-all-start) | async-done | bytes 655392 | tf_op jit(solution)/shard_map/all_to_all | solution.py:255
  42.7 0.1 reshape.22
  42.8 0.2 reshape.20
  43.1 0.3 convolution_convert_fusion
  43.4 1.1 %broadcast_in_dim.9 = bf16[4,8,16,1152]{3,2,1,0:T(8,128)(2,1)} broadcast(bf16[8,16,1152]{2,1,0:T(8,128)(2,1)S(1)} %bitcast.14), dimensions={1,2,3} | broadcast | bytes 1474560 | tf_op jit(solution)/shard_map/broadcast_in_dim | solution.py:275
  44.5 0.0 copy-start.1
  44.5 7.0 %all-to-all-start.1 = ((bf16[32,16,1152]{2,1,0:T(8,128)(2,1)}), bf16[32,16,1152]{2,1,0:T(8,128)(2,1)S(1)}, u32[]{:S(2)}, u32[]{:S(2)}) async-start(bf16[32,16,1152]{2,1,0:T(8,128)(2,1)} %bitcast.4), calls=%async_computation.1 | async-start | bytes 2359296 | tf_op jit(solution)/shard_map/all_to_all | solution.py:274
  51.5 0.0 copy-done.1
  51.5 5.1 %shard_map.46 = (bf16[8,128,576]{2,1,0:T(8,128)(2,1)S(1)}, bf16[8,128,576]{2,1,0:T(8,128)(2,1)S(1)}, s32[2,1,512]{2,1,0:T(1,128)S(1)}) custom-call(s32[2,8]{1,0:T(2,128)S(1)} %copy-done.1, bf16[16,576,128]{2,1,0:T(8,128)(2,1)} %bitcast.16), custom_call_target="tpu_custom_call" | custom-call | flops 1000000000 | bytes 10485760 | tf_op jit(solution)/shard_map/pallas_call | solution.py:217
  56.5 0.0 copy-start
  56.6 1.1 %copy-done = bf16[8,128,576]{2,1,0:T(8,128)(2,1)} copy-done((bf16[8,128,576]{2,1,0:T(8,128)(2,1)}, bf16[8,128,576]{2,1,0:T(8,128)(2,1)S(1)}, u32[]{:S(2)}) %copy-start) | copy-done | bytes 1179672
  57.6 12.0 %all-to-all-done.1.k_ref = bf16[32,16,1152]{2,1,0:T(8,128)(2,1)S(1)} async-done(((bf16[32,16,1152]{2,1,0:T(8,128)(2,1)}), bf16[32,16,1152]{2,1,0:T(8,128)(2,1)S(1)}, u32[]{:S(2)}, u32[]{:S(2)}) %all-to-all-start.1) | async-done | bytes 1179680 | tf_op jit(solution)/shard_map/all_to_all | solution.py:274
  69.6 5.3 %shard_map.48 = bf16[128,2048]{1,0:T(8,128)(2,1)S(1)} custom-call(bf16[8,128,576]{2,1,0:T(8,128)(2,1)S(1)} %get-tuple-element.8.low_ref, bf16[8,128,576]{2,1,0:T(8,128)(2,1)} %copy-done, bf16[32,16,1152]{2,1,0:T(8,128)(2,1)S(1)} %all-to-all-done.1.k_ref, s32[2,1,512]{2,1,0:T(1,128)S(1)} %get-tuple-element.10.place_ref, bf16[16,512,128]{2,1,0:T(8,128)(2,1)} %w_hbm.1), custom_call_target="tpu_custom_call" | custom-call | tf_op jit(solution)/shard_map/pallas_call | solution.py:95
  74.9 11.8 %all_to_all.29 = bf16[4,32,2048]{2,1,0:T(8,128)(2,1)S(1)} all-to-all(bf16[4,32,2048]{2,1,0:T(8,128)(2,1)S(1)} %bitcast.11), channel_id=1, replica_groups=mesh['ctx'=128,'head'=4] {'head'}, dimensions={0} | all-to-all | bytes 1048576 | tf_op jit(solution)/shard_map/all_to_all | solution.py:285
  86.7 0.8 copy.17
  (4 shorter events, 0.1 us)
Async XLA Ops:
  2.0 40.6 %all-to-all-start = ((bf16[128,2,1280]{2,1,0:T(2,128)(2,1)}), bf16[128,2,1280]{2,1,0:T(2,128)(2,1)S(1)}, u32[]{:S(2)}, u32[]{:S(2)}) async-start(bf16[128,2,1280]{2,1,0:T(2,128)(2,1)} %bitcast.12), calls=%async_computation | async-start | bytes 1310720 | tf_op jit(solution)/shard_map/all_to_all | solution.py:255
  44.5 7.0 %copy-start.1 = (s32[2,8]{1,0:T(2,128)S(1)}, s32[2,8]{1,0:T(2,128)}, u32[]{:S(2)}) copy-start(s32[2,8]{1,0:T(2,128)} %selected_hbm.1) | copy-start | bytes 196
  44.5 25.1 %all-to-all-start.1 = ((bf16[32,16,1152]{2,1,0:T(8,128)(2,1)}), bf16[32,16,1152]{2,1,0:T(8,128)(2,1)S(1)}, u32[]{:S(2)}, u32[]{:S(2)}) async-start(bf16[32,16,1152]{2,1,0:T(8,128)(2,1)} %bitcast.4), calls=%async_computation.1 | async-start | bytes 2359296 | tf_op jit(solution)/shard_map/all_to_all | solution.py:274
  56.5 1.1 %copy-start = (bf16[8,128,576]{2,1,0:T(8,128)(2,1)}, bf16[8,128,576]{2,1,0:T(8,128)(2,1)S(1)}, u32[]{:S(2)}) copy-start(bf16[8,128,576]{2,1,0:T(8,128)(2,1)S(1)} %get-tuple-element.9.high_hbm) | copy-start | bytes 3538948

commit v5 on v4

--- a/solution.py
+++ b/solution.py
@@ -4,6 +4,7 @@
 from jax.experimental import pallas as pl
 from jax.experimental.pallas import tpu as pltpu
 from jax.sharding import PartitionSpec as P
+
 
 DC = 512
 DR = 64
@@ -18,10 +19,10 @@
 FACTOR = (DV + DR) ** -0.5 * 1.4426950408889634
 
 
-def attend_kernel(low_ref, high_hbm, k_ref, place_ref, w_hbm, o_ref, keys_ref, high_ref, w_ref, sems):
-    part, tokens, width = low_ref.shape
-    heads = w_ref.shape[0]
-    bands, per_band, _ = k_ref.shape
+def attend_kernel(q_ref, k_ref, place_ref, w_hbm, o_ref, keys_ref, w_ref, sems):
+    heads, tokens, width = q_ref.shape
+    part = heads // 2
+    bands, _, _ = k_ref.shape
     blocks = tokens // KBLK
     half = bands * SEL
     count = BAND_TOKENS * half
@@ -29,8 +30,7 @@
     low, high = pl.ds(0, part), pl.ds(part, part)
     copies = [
         pltpu.make_async_copy(w_hbm.at[low], w_ref.at[low], sems.at[0]),
-        pltpu.make_async_copy(high_hbm, high_ref, sems.at[1]),
-        pltpu.make_async_copy(w_hbm.at[high], w_ref.at[high], sems.at[2]),
+        pltpu.make_async_copy(w_hbm.at[high], w_ref.at[high], sems.at[1]),
     ]
     for copy in copies:
         copy.start()
@@ -46,7 +46,7 @@
 
     def score(group, block):
         here = slice(block * KBLK, (block + 1) * KBLK)
-        queries = (high_ref if group else low_ref)[:, here, :].reshape(part * KBLK, width)
+        queries = q_ref[group * part : (group + 1) * part, here, :].reshape(part * KBLK, width)
         return lax.dot_general(
             queries, keys_ref[block], (((1,), (1,)), ((), ())), preferred_element_type=jnp.float32
         )
@@ -63,7 +63,7 @@
             preferred_element_type=jnp.float32,
         ).astype(jnp.bfloat16)
         if block == 0:
-            copies[2 if group else 0].wait()
+            copies[group].wait()
         for index in range(part):
             head = group * part + index
             columns = slice(head * DV, (head + 1) * DV)
@@ -77,8 +77,6 @@
     waiting = None
     for group in range(heads // part):
         for block in range(blocks):
-            if group and block == 0:
-                copies[1].wait()
             scores = score(group, block)
             if waiting is not None:
                 finish(*waiting)
@@ -86,31 +84,22 @@
     finish(*waiting)
 
 
-def attend(low, high, keys, place, value_weight):
-    part, tokens, width = low.shape
-    heads = value_weight.shape[0]
+def attend(queries, keys, place, value_weight):
+    heads, tokens, width = queries.shape
     blocks = tokens // KBLK
     vmem = pl.BlockSpec(memory_space=pltpu.VMEM)
-    hbm = pl.BlockSpec(memory_space=pltpu.HBM)
     return pl.pallas_call(
         attend_kernel,
         out_shape=jax.ShapeDtypeStruct((tokens, heads * DV), jnp.bfloat16),
-        in_specs=[vmem, hbm, vmem, vmem, hbm],
+        in_specs=[vmem, vmem, vmem, pl.BlockSpec(memory_space=pltpu.HBM)],
         out_specs=vmem,
         scratch_shapes=[
             pltpu.VMEM((blocks, SEL * KBLK, width), jnp.bfloat16),
-            pltpu.VMEM(high.shape, high.dtype),
             pltpu.VMEM(value_weight.shape, value_weight.dtype),
-            pltpu.SemaphoreType.DMA((3,)),
+            pltpu.SemaphoreType.DMA((2,)),
         ],
         compiler_params=pltpu.CompilerParams(vmem_limit_bytes=32 * 2**20),
-    )(
-        low,
-        pltpu.with_memory_space_constraint(high, pltpu.HBM),
-        keys,
-        place,
-        pltpu.with_memory_space_constraint(value_weight, pltpu.HBM),
-    )
+    )(queries, keys, place, pltpu.with_memory_space_constraint(value_weight, pltpu.HBM))
 
 
 def spread_kernel(selected_hbm, latent_hbm, out_hbm, band_ref, selected_ref, in_sem, out_sem):
@@ -169,9 +158,8 @@
     )
 
 
-def stage_kernel(selected_ref, raw_hbm, low_ref, high_hbm, place_ref, raw_ref, high_ref, sems, out_sem):
+def stage_kernel(selected_ref, raw_hbm, q_ref, place_ref, raw_ref, sems):
     heads, _, tokens = raw_ref.shape
-    part = low_ref.shape[0]
     copies = []
     for head in range(heads):
         copy = pltpu.make_async_copy(raw_hbm.at[head], raw_ref.at[head], sems.at[head])
@@ -198,14 +186,8 @@
         copies[head].wait()
         turned = lax.dot_general(
             unit, raw_ref[head], (((1,), (1,)), ((), ())), preferred_element_type=jnp.float32
-        ).astype(jnp.bfloat16)
-        if head < part:
-            low_ref[head] = turned
-        else:
-            high_ref[head - part] = turned
-    copy = pltpu.make_async_copy(high_ref, high_hbm, out_sem)
-    copy.start()
-    copy.wait()
+        )
+        q_ref[head] = turned.astype(jnp.bfloat16)
 
 
 def stage(selected, queries):
@@ -213,21 +195,46 @@
     blocks = selected.shape[0]
     hbm = pl.BlockSpec(memory_space=pltpu.HBM)
     vmem = pl.BlockSpec(memory_space=pltpu.VMEM)
-    group = jax.ShapeDtypeStruct((heads // 2, tokens, width), queries.dtype)
     return pl.pallas_call(
         stage_kernel,
-        out_shape=(group, group, jax.ShapeDtypeStruct((blocks, 1, SEL * KBLK), jnp.int32)),
+        out_shape=(
+            jax.ShapeDtypeStruct((heads, tokens, width), queries.dtype),
+            jax.ShapeDtypeStruct((blocks, 1, SEL * KBLK), jnp.int32),
+        ),
         in_specs=[pl.BlockSpec(memory_space=pltpu.SMEM), hbm],
-        out_specs=(vmem, hbm, vmem),
+        out_specs=(vmem, vmem),
         scratch_shapes=[
             pltpu.VMEM((heads, width, tokens), queries.dtype),
-            pltpu.VMEM(group.shape, queries.dtype),
             pltpu.SemaphoreType.DMA((heads,)),
-            pltpu.SemaphoreType.DMA,
         ],
         compiler_params=pltpu.CompilerParams(vmem_limit_bytes=16 * 2**20),
         cost_estimate=pl.CostEstimate(flops=10**9, transcendentals=0, bytes_accessed=10 * 2**20),
     )(selected, pltpu.with_memory_space_constraint(queries.transpose(1, 2, 0), pltpu.HBM))
+
+
+def pick_kernel(wanted_ref, table_ref, out_ref):
+    blocks = table_ref.shape[0] * table_ref.shape[1]
+    table = table_ref[:, :, :BAND].reshape(blocks, BAND)
+    chosen = wanted_ref[...] == lax.broadcasted_iota(jnp.int32, (blocks, 1), 0)
+    picked = lax.dot_general(
+        chosen.astype(jnp.float32).astype(jnp.bfloat16),
+        table,
+        (((0,), (0,)), ((), ())),
+        preferred_element_type=jnp.float32,
+    ).astype(jnp.bfloat16)
+    for head in range(out_ref.shape[0]):
+        out_ref[head] = picked
+
+
+def pick(wanted, table, heads):
+    vmem = pl.BlockSpec(memory_space=pltpu.VMEM)
+    return pl.pallas_call(
+        pick_kernel,
+        out_shape=jax.ShapeDtypeStruct((heads, wanted.shape[1], BAND), table.dtype),
+        in_specs=[vmem, vmem],
+        out_specs=vmem,
+        compiler_params=pltpu.CompilerParams(vmem_limit_bytes=16 * 2**20),
+    )(wanted, table)
 
 
 def fetch_groups(heads):
@@ -259,29 +266,21 @@
         concat_axis=0,
         tiled=True,
     )
-    table = spread.reshape(ctx_size * here, ROW)
-
+    turned, place = stage(selected, queries)
     lists = spread[:, :, BAND : BAND + SEL].reshape(Y // 2, 2, Z // 2, 2, CORES, here, SEL)
     y, z = ctx // (Z * CORES), (ctx // CORES) % Z
     lists = lax.dynamic_slice_in_dim(lists, y // 2, 1, 0)
     lists = lax.dynamic_slice_in_dim(lists, z // 2, 1, 2)
     wanted = lists.astype(jnp.int32).reshape(-1)
-    chosen = wanted[:, None] == jnp.arange(ctx_size * here, dtype=jnp.int32)[None, :]
-    picked = jnp.dot(
-        chosen.astype(jnp.bfloat16), table[:, :BAND], preferred_element_type=jnp.float32
-    ).astype(jnp.bfloat16)
-    picked = picked.reshape(1, cell, here * SEL, BAND)
     keys = lax.all_to_all(
-        jnp.broadcast_to(picked, (heads, cell, here * SEL, BAND)).reshape(bands, here * SEL, BAND),
+        pick(wanted.reshape(1, -1), spread, heads).reshape(bands, here * SEL, BAND),
         ("ctx", "head"),
         split_axis=0,
         concat_axis=0,
         axis_index_groups=fetch_groups(heads),
         tiled=True,
     )
-
-    low, high, place = stage(selected, queries)
-    attended = attend(low, high, keys, place, value_weight)
+    attended = attend(turned, keys, place, value_weight)
     return lax.all_to_all(attended, "head", split_axis=0, concat_axis=1, tiled=True)
 
 

time: 87.9 us -> 88.2 us (level)
    unnamed x5 -> x6, local copies, waits for them, and re-layouts: 1.09 us -> 3.26 us
    pallas_call x1 -> x2, Pallas kernels: 5.08 us -> 6.31 us  [the longest x1 4.97 us: stage(): pl.pallas_call(stage_kernel, out_shape=(jax.ShapeDtypeStruct((heads, toke...]
    broadcast_in_dim x1 -> x0, local copies, waits for them, and re-layouts: 1.1 us -> none  [per_device(): jnp.broadcast_to(picked, (heads, cell, here * SEL, BAND))]
    pallas_call x1, Pallas kernels: 5.32 us -> 4.35 us  [attend(): pl.pallas_call(attend_kernel, out_shape=jax.ShapeDtypeStruct((tokens, hea...]
where the time goes in v5:
time: 88.2 us; the launch traced here: 87.8 us
  waiting for transfers between devices  33.7 us (38%)
  starting transfers between devices  25.2 us (29%)
  Pallas kernels  12.7 us (14%)
  blocking collectives  11.8 us (13%)
  local copies, waits for them, and re-layouts  4.23 us (5%)
    all_to_all x1, waiting for transfers between devices, per_device(): lax.all_to_all(spread_bands(selected, latent_cache).reshape(ctx_size, her...  22.1 us
    all_to_all x1, starting transfers between devices, per_device(): lax.all_to_all(spread_bands(selected, latent_cache).reshape(ctx_size, her...  18.4 us
    all_to_all x1, blocking collectives, per_device(): lax.all_to_all(attended, 'head', split_axis=0, concat_axis=1, tiled=True)  11.8 us
    all_to_all x1, waiting for transfers between devices, per_device(): lax.all_to_all(pick(wanted.reshape(1, -1), spread, heads).reshape(bands,...  11.6 us
    all_to_all x1, starting transfers between devices, per_device(): lax.all_to_all(pick(wanted.reshape(1, -1), spread, heads).reshape(bands,...  6.83 us
    pallas_call x1, Pallas kernels, stage(): pl.pallas_call(stage_kernel, out_shape=(jax.ShapeDtypeStruct((heads, toke...  4.97 us
    pallas_call x1, Pallas kernels, attend(): pl.pallas_call(attend_kernel, out_shape=jax.ShapeDtypeStruct((tokens, hea...  4.35 us
    unnamed x6, local copies, waits for them, and re-layouts  3.26 us
  transfers between devices with their start and end apart: 2, of which 2 were waited for; matrix products, arithmetic and copies ran while one was open for 0% of the time, Pallas kernels for 6%

profile of v5, /device:TPU:1, one launch (start us, length us, event | category | flops | bytes accessed | tf_op | source)
XLA Modules:
  0.0 87.8 jit_solution(14963947526727493113)
XLA Ops:
  0.0 2.0 %shard_map.47 = bf16[4,2,4,4,2,1280]{5,4,3,2,1,0:T(2,128)(2,1)} custom-call(s32[2,8]{1,0:T(2,128)} %selected_hbm.1, bf16[2,36864]{1,0:T(2,128)(2,1)} %latent_hbm.1), custom_call_target="tpu_custom_call" | custom-call | tf_op jit(solution)/shard_map/pallas_call | solution.py:144
  2.0 18.4 %all-to-all-start = ((bf16[128,2,1280]{2,1,0:T(2,128)(2,1)}), bf16[128,2,1280]{2,1,0:T(2,128)(2,1)S(1)}, u32[]{:S(2)}, u32[]{:S(2)}) async-start(bf16[128,2,1280]{2,1,0:T(2,128)(2,1)} %bitcast.13), calls=%async_computation | async-start | bytes 1310720 | tf_op jit(solution)/shard_map/all_to_all | solution.py:262
  20.5 22.1 %all-to-all-done.table_ref = bf16[128,2,1280]{2,1,0:T(2,128)(2,1)S(1)} async-done(((bf16[128,2,1280]{2,1,0:T(2,128)(2,1)}), bf16[128,2,1280]{2,1,0:T(2,128)(2,1)S(1)}, u32[]{:S(2)}, u32[]{:S(2)}) %all-to-all-start) | async-done | bytes 655392 | tf_op jit(solution)/shard_map/all_to_all | solution.py:262
  42.7 0.1 reshape.15.wanted_ref
  42.8 0.0 copy-start.2
  42.8 1.3 %shard_map.48 = bf16[4,128,1152]{2,1,0:T(8,128)(2,1)} custom-call(s32[1,128]{1,0:T(1,128)S(1)} %reshape.15.wanted_ref, bf16[128,2,1280]{2,1,0:T(2,128)(2,1)S(1)} %all-to-all-done.table_ref), custom_call_target="tpu_custom_call" | custom-call | tf_op jit(solution)/shard_map/pallas_call | solution.py:231
  44.1 6.8 %all-to-all-start.1 = ((bf16[32,16,1152]{2,1,0:T(8,128)(2,1)}), bf16[32,16,1152]{2,1,0:T(8,128)(2,1)S(1)}, u32[]{:S(2)}, u32[]{:S(2)}) async-start(bf16[32,16,1152]{2,1,0:T(8,128)(2,1)} %bitcast.3), calls=%async_computation.1 | async-start | bytes 2359296 | tf_op jit(solution)/shard_map/all_to_all | solution.py:275
  51.0 0.0 copy-done.2
  51.0 5.0 %shard_map.46 = (bf16[16,128,576]{2,1,0:T(8,128)(2,1)S(1)}, s32[2,1,512]{2,1,0:T(1,128)S(1)}) custom-call(s32[2,8]{1,0:T(2,128)S(1)} %copy-done.2, bf16[16,576,128]{2,1,0:T(8,128)(2,1)} %bitcast.16), custom_call_target="tpu_custom_call" | custom-call | flops 1000000000 | bytes 10485760 | tf_op jit(solution)/shard_map/pallas_call | solution.py:198
  56.0 0.0 copy-start
  56.0 1.5 %copy-done = bf16[16,128,576]{2,1,0:T(8,128)(2,1)} copy-done((bf16[16,128,576]{2,1,0:T(8,128)(2,1)}, bf16[16,128,576]{2,1,0:T(8,128)(2,1)S(1)}, u32[]{:S(2)}) %copy-start) | copy-done | bytes 2359320
  57.5 11.6 %all-to-all-done.1.k_ref = bf16[32,16,1152]{2,1,0:T(8,128)(2,1)S(1)} async-done(((bf16[32,16,1152]{2,1,0:T(8,128)(2,1)}), bf16[32,16,1152]{2,1,0:T(8,128)(2,1)S(1)}, u32[]{:S(2)}, u32[]{:S(2)}) %all-to-all-start.1) | async-done | bytes 1179680 | tf_op jit(solution)/shard_map/all_to_all | solution.py:275
  69.1 0.0 copy-start.1
  69.1 1.7 %copy-done.1 = bf16[16,128,576]{2,1,0:T(8,128)(2,1)S(1)} copy-done((bf16[16,128,576]{2,1,0:T(8,128)(2,1)S(1)}, bf16[16,128,576]{2,1,0:T(8,128)(2,1)}, u32[]{:S(2)}) %copy-start.1) | copy-done | bytes 2359320
  70.9 4.3 %shard_map.49 = bf16[128,2048]{1,0:T(8,128)(2,1)S(1)} custom-call(bf16[16,128,576]{2,1,0:T(8,128)(2,1)S(1)} %copy-done.1, bf16[32,16,1152]{2,1,0:T(8,128)(2,1)S(1)} %all-to-all-done.1.k_ref, s32[2,1,512]{2,1,0:T(1,128)S(1)} %get-tuple-element.8.place_ref, bf16[16,512,128]{2,1,0:T(8,128)(2,1)} %w_hbm.1), custom_call_target="tpu_custom_call" | custom-call | tf_op jit(solution)/shard_map/pallas_call | solution.py:91
  75.2 11.8 %all_to_all.29 = bf16[4,32,2048]{2,1,0:T(8,128)(2,1)S(1)} all-to-all(bf16[4,32,2048]{2,1,0:T(8,128)(2,1)S(1)} %bitcast.12), channel_id=1, replica_groups=mesh['ctx'=128,'head'=4] {'head'}, dimensions={0} | all-to-all | bytes 1048576 | tf_op jit(solution)/shard_map/all_to_all | solution.py:284
  87.0 0.8 copy.8
  (2 shorter events, 0.1 us)
Async XLA Ops:
  2.0 40.6 %all-to-all-start = ((bf16[128,2,1280]{2,1,0:T(2,128)(2,1)}), bf16[128,2,1280]{2,1,0:T(2,128)(2,1)S(1)}, u32[]{:S(2)}, u32[]{:S(2)}) async-start(bf16[128,2,1280]{2,1,0:T(2,128)(2,1)} %bitcast.13), calls=%async_computation | async-start | bytes 1310720 | tf_op jit(solution)/shard_map/all_to_all | solution.py:262
  42.8 8.2 %copy-start.2 = (s32[2,8]{1,0:T(2,128)S(1)}, s32[2,8]{1,0:T(2,128)}, u32[]{:S(2)}) copy-start(s32[2,8]{1,0:T(2,128)} %selected_hbm.1) | copy-start | bytes 196
  44.1 25.0 %all-to-all-start.1 = ((bf16[32,16,1152]{2,1,0:T(8,128)(2,1)}), bf16[32,16,1152]{2,1,0:T(8,128)(2,1)S(1)}, u32[]{:S(2)}, u32[]{:S(2)}) async-start(bf16[32,16,1152]{2,1,0:T(8,128)(2,1)} %bitcast.3), calls=%async_computation.1 | async-start | bytes 2359296 | tf_op jit(solution)/shard_map/all_to_all | solution.py:275
  56.0 1.5 %copy-start = (bf16[16,128,576]{2,1,0:T(8,128)(2,1)}, bf16[16,128,576]{2,1,0:T(8,128)(2,1)S(1)}, u32[]{:S(2)}) copy-start(bf16[16,128,576]{2,1,0:T(8,128)(2,1)S(1)} %get-tuple-element.7.q_ref) | copy-start | bytes 7077892
  69.1 1.7 %copy-start.1 = (bf16[16,128,576]{2,1,0:T(8,128)(2,1)S(1)}, bf16[16,128,576]{2,1,0:T(8,128)(2,1)}, u32[]{:S(2)}) copy-start(bf16[16,128,576]{2,1,0:T(8,128)(2,1)} %copy-done) | copy-start | bytes 7077892

commit v6 on v5

--- a/solution.py
+++ b/solution.py
@@ -14,18 +14,22 @@
 WIDTH = DC + DR
 BAND_TOKENS = 2
 BAND = BAND_TOKENS * WIDTH
-ROW = BAND + 128
+LANES = 128
+ROW = BAND + LANES
 Y, Z, CORES = 8, 8, 2
 FACTOR = (DV + DR) ** -0.5 * 1.4426950408889634
 
 
-def attend_kernel(q_ref, k_ref, place_ref, w_hbm, o_ref, keys_ref, w_ref, sems):
+def attend_kernel(
+    q_ref, k_ref, own_ref, place_ref, w_hbm, o_ref, keys_ref, w_ref, plain_ref, wide_ref, sems
+):
     heads, tokens, width = q_ref.shape
     part = heads // 2
-    bands, _, _ = k_ref.shape
+    bands = k_ref.shape[0]
     blocks = tokens // KBLK
     half = bands * SEL
     count = BAND_TOKENS * half
+    others = SEL - 1
 
     low, high = pl.ds(0, part), pl.ds(part, part)
     copies = [
@@ -35,12 +39,23 @@
     for copy in copies:
         copy.start()
 
+    plain_ref[...] = k_ref[...].astype(jnp.float32)
     biases = []
     for block in range(blocks):
-        picked = slice(block * SEL, (block + 1) * SEL)
+        for tile in range(BAND // LANES):
+            first = (tile * blocks + block) * others
+            rows = plain_ref[:, first : first + SEL, :].reshape(half, LANES)
+            wide_ref[tile * half : (tile + 1) * half, :] = rows
+            wide_ref[pl.ds(tile * half + others, bands, stride=SEL), :] = own_ref[
+                block, :, tile * LANES : (tile + 1) * LANES
+            ]
+        whole = jnp.concatenate(
+            [wide_ref[tile * half : (tile + 1) * half, :] for tile in range(BAND // LANES)], axis=1
+        ).astype(jnp.bfloat16)
         for token in range(BAND_TOKENS):
-            rows = k_ref[:, picked, token * width : (token + 1) * width]
-            keys_ref[block, token * half : (token + 1) * half, :] = rows.reshape(half, width)
+            keys_ref[block, token * half : (token + 1) * half, :] = whole[
+                :, token * width : (token + 1) * width
+            ]
         query_place = lax.broadcasted_iota(jnp.int32, (KBLK, 1), 0)
         biases.append(jnp.where(place_ref[block] <= query_place, 0.0, -1e30))
 
@@ -84,22 +99,24 @@
     finish(*waiting)
 
 
-def attend(queries, keys, place, value_weight):
+def attend(queries, keys, own, place, value_weight):
     heads, tokens, width = queries.shape
     blocks = tokens // KBLK
     vmem = pl.BlockSpec(memory_space=pltpu.VMEM)
     return pl.pallas_call(
         attend_kernel,
         out_shape=jax.ShapeDtypeStruct((tokens, heads * DV), jnp.bfloat16),
-        in_specs=[vmem, vmem, vmem, pl.BlockSpec(memory_space=pltpu.HBM)],
+        in_specs=[vmem, vmem, vmem, vmem, pl.BlockSpec(memory_space=pltpu.HBM)],
         out_specs=vmem,
         scratch_shapes=[
             pltpu.VMEM((blocks, SEL * KBLK, width), jnp.bfloat16),
             pltpu.VMEM(value_weight.shape, value_weight.dtype),
+            pltpu.VMEM(keys.shape, jnp.float32),
+            pltpu.VMEM((BAND // LANES * keys.shape[0] * SEL, LANES), jnp.float32),
             pltpu.SemaphoreType.DMA((2,)),
         ],
         compiler_params=pltpu.CompilerParams(vmem_limit_bytes=32 * 2**20),
-    )(queries, keys, place, pltpu.with_memory_space_constraint(value_weight, pltpu.HBM))
+    )(queries, keys, own, place, pltpu.with_memory_space_constraint(value_weight, pltpu.HBM))
 
 
 def spread_kernel(selected_hbm, latent_hbm, out_hbm, band_ref, selected_ref, in_sem, out_sem):
@@ -158,8 +175,12 @@
     )
 
 
-def stage_kernel(selected_ref, raw_hbm, q_ref, place_ref, raw_ref, sems):
+def stage_kernel(
+    selected_ref, raw_hbm, latent_hbm, q_ref, place_ref, own_ref, raw_ref, latent_ref, sems, own_sem
+):
     heads, _, tokens = raw_ref.shape
+    own_copy = pltpu.make_async_copy(latent_hbm, latent_ref, own_sem)
+    own_copy.start()
     copies = []
     for head in range(heads):
         copy = pltpu.make_async_copy(raw_hbm.at[head], raw_ref.at[head], sems.at[head])
@@ -174,7 +195,8 @@
     for block in range(blocks):
         chosen = jnp.full((1, count), -1, jnp.int32)
         for index in range(SEL):
-            chosen = jnp.where(slot == index, selected_ref[block, index], chosen)
+            position = (index + SEL - 1) % SEL
+            chosen = jnp.where(slot == position, selected_ref[block, index], chosen)
         own = lax.axis_index("ctx") * blocks + block
         place_ref[block] = jnp.where(chosen >= 0, (chosen - own) * KBLK + offset, 2**30)
 
@@ -188,9 +210,14 @@
             unit, raw_ref[head], (((1,), (1,)), ((), ())), preferred_element_type=jnp.float32
         )
         q_ref[head] = turned.astype(jnp.bfloat16)
-
-
-def stage(selected, queries):
+    own_copy.wait()
+    for band in range(own_ref.shape[1]):
+        rows = latent_ref[:, band * BAND : (band + 1) * BAND].astype(jnp.float32)
+        for block in range(blocks):
+            own_ref[block, band : band + 1, :] = rows[block : block + 1]
+
+
+def stage(selected, queries, latent_cache):
     tokens, heads, width = queries.shape
     blocks = selected.shape[0]
     hbm = pl.BlockSpec(memory_space=pltpu.HBM)
@@ -200,20 +227,28 @@
         out_shape=(
             jax.ShapeDtypeStruct((heads, tokens, width), queries.dtype),
             jax.ShapeDtypeStruct((blocks, 1, SEL * KBLK), jnp.int32),
+            jax.ShapeDtypeStruct((blocks, KBLK // BAND_TOKENS, BAND), jnp.float32),
         ),
-        in_specs=[pl.BlockSpec(memory_space=pltpu.SMEM), hbm],
-        out_specs=(vmem, vmem),
+        in_specs=[pl.BlockSpec(memory_space=pltpu.SMEM), hbm, hbm],
+        out_specs=(vmem, vmem, vmem),
         scratch_shapes=[
             pltpu.VMEM((heads, width, tokens), queries.dtype),
+            pltpu.VMEM(latent_cache.shape, latent_cache.dtype),
             pltpu.SemaphoreType.DMA((heads,)),
+            pltpu.SemaphoreType.DMA,
         ],
         compiler_params=pltpu.CompilerParams(vmem_limit_bytes=16 * 2**20),
         cost_estimate=pl.CostEstimate(flops=10**9, transcendentals=0, bytes_accessed=10 * 2**20),
-    )(selected, pltpu.with_memory_space_constraint(queries.transpose(1, 2, 0), pltpu.HBM))
-
-
-def pick_kernel(wanted_ref, table_ref, out_ref):
+    )(
+        selected,
+        pltpu.with_memory_space_constraint(queries.transpose(1, 2, 0), pltpu.HBM),
+        pltpu.with_memory_space_constraint(latent_cache, pltpu.HBM),
+    )
+
+
+def pick_kernel(wanted_ref, table_ref, out_ref, packed_ref):
     blocks = table_ref.shape[0] * table_ref.shape[1]
+    heads, cell, rows, _ = out_ref.shape
     table = table_ref[:, :, :BAND].reshape(blocks, BAND)
     chosen = wanted_ref[...] == lax.broadcasted_iota(jnp.int32, (blocks, 1), 0)
     picked = lax.dot_general(
@@ -221,18 +256,33 @@
         table,
         (((0,), (0,)), ((), ())),
         preferred_element_type=jnp.float32,
-    ).astype(jnp.bfloat16)
-    for head in range(out_ref.shape[0]):
-        out_ref[head] = picked
+    )
+    tiles = BAND // LANES
+    count = rows // tiles
+    step = picked.shape[0] // cell
+    packed_ref[:, tiles * count :, :] = jnp.zeros((cell, rows - tiles * count, LANES), jnp.float32)
+    for place in range(cell):
+        for tile in range(tiles):
+            packed_ref[place, tile * count : (tile + 1) * count, :] = picked[
+                place * step : place * step + count, tile * LANES : (tile + 1) * LANES
+            ]
+    packed = packed_ref[...].astype(out_ref.dtype)
+    for head in range(heads):
+        out_ref[head] = packed
 
 
 def pick(wanted, table, heads):
+    cell, count = wanted.shape
+    step = -(-count // 8) * 8
+    rows = -(-count * (BAND // LANES) // 8) * 8
+    wanted = jnp.pad(wanted, ((0, 0), (0, step - count)), constant_values=-1).reshape(1, -1)
     vmem = pl.BlockSpec(memory_space=pltpu.VMEM)
     return pl.pallas_call(
         pick_kernel,
-        out_shape=jax.ShapeDtypeStruct((heads, wanted.shape[1], BAND), table.dtype),
+        out_shape=jax.ShapeDtypeStruct((heads, cell, rows, LANES), table.dtype),
         in_specs=[vmem, vmem],
         out_specs=vmem,
+        scratch_shapes=[pltpu.VMEM((cell, rows, LANES), jnp.float32)],
         compiler_params=pltpu.CompilerParams(vmem_limit_bytes=16 * 2**20),
     )(wanted, table)
 
@@ -266,21 +316,22 @@
         concat_axis=0,
         tiled=True,
     )
-    turned, place = stage(selected, queries)
+    turned, place, own = stage(selected, queries, latent_cache)
     lists = spread[:, :, BAND : BAND + SEL].reshape(Y // 2, 2, Z // 2, 2, CORES, here, SEL)
     y, z = ctx // (Z * CORES), (ctx // CORES) % Z
     lists = lax.dynamic_slice_in_dim(lists, y // 2, 1, 0)
     lists = lax.dynamic_slice_in_dim(lists, z // 2, 1, 2)
-    wanted = lists.astype(jnp.int32).reshape(-1)
+    wanted = lists.astype(jnp.int32)[..., 1:].reshape(cell, -1)
+    rows = pick(wanted, spread, heads)
     keys = lax.all_to_all(
-        pick(wanted.reshape(1, -1), spread, heads).reshape(bands, here * SEL, BAND),
+        rows.reshape(bands, rows.shape[2], LANES),
         ("ctx", "head"),
         split_axis=0,
         concat_axis=0,
         axis_index_groups=fetch_groups(heads),
         tiled=True,
     )
-    attended = attend(turned, keys, place, value_weight)
+    attended = attend(turned, keys, own, place, value_weight)
     return lax.all_to_all(attended, "head", split_axis=0, concat_axis=1, tiled=True)
 
 

time: 88.2 us -> 87.6 us (level)
  waiting for transfers between devices: 33.7 us -> 32.2 us
    all_to_all x1, waiting for transfers between devices: 11.6 us -> 10.2 us  [per_device(): lax.all_to_all(rows.reshape(bands, rows.shape[2], LANES), ('ctx', 'head')...]
    unnamed x6 -> x7, local copies, waits for them, and re-layouts: 3.26 us -> 3.34 us
where the time goes in v6:
time: 87.6 us; the launch traced here: 87.3 us
  waiting for transfers between devices  32.2 us (37%)
  starting transfers between devices  25.2 us (29%)
  Pallas kernels  13.2 us (15%)
  blocking collectives  12 us (14%)
  local copies, waits for them, and re-layouts  4.4 us (5%)
    all_to_all x1, waiting for transfers between devices, per_device(): lax.all_to_all(spread_bands(selected, latent_cache).reshape(ctx_size, her...  22.1 us
    all_to_all x1, starting transfers between devices, per_device(): lax.all_to_all(spread_bands(selected, latent_cache).reshape(ctx_size, her...  18.4 us
    all_to_all x1, blocking collectives, per_device(): lax.all_to_all(attended, 'head', split_axis=0, concat_axis=1, tiled=True)  12 us
    all_to_all x1, waiting for transfers between devices, per_device(): lax.all_to_all(rows.reshape(bands, rows.shape[2], LANES), ('ctx', 'head')...  10.2 us
    all_to_all x1, starting transfers between devices, per_device(): lax.all_to_all(rows.reshape(bands, rows.shape[2], LANES), ('ctx', 'head')...  6.82 us
    pallas_call x1, Pallas kernels, stage(): pl.pallas_call(stage_kernel, out_shape=(jax.ShapeDtypeStruct((heads, toke...  5.04 us
    pallas_call x1, Pallas kernels, attend(): pl.pallas_call(attend_kernel, out_shape=jax.ShapeDtypeStruct((tokens, hea...  4.84 us
    unnamed x7, local copies, waits for them, and re-layouts  3.34 us
  transfers between devices with their start and end apart: 2, of which 2 were waited for; matrix products, arithmetic and copies ran while one was open for 0% of the time, Pallas kernels for 6%

profile of v6, /device:TPU:1, one launch (start us, length us, event | category | flops | bytes accessed | tf_op | source)
XLA Modules:
  0.0 87.3 jit_solution(6877977657283463293)
XLA Ops:
  0.0 2.0 %shard_map.47 = bf16[4,2,4,4,2,1280]{5,4,3,2,1,0:T(2,128)(2,1)} custom-call(s32[2,8]{1,0:T(2,128)} %selected_hbm.1, bf16[2,36864]{1,0:T(2,128)(2,1)} %latent_hbm.3), custom_call_target="tpu_custom_call" | custom-call | tf_op jit(solution)/shard_map/pallas_call | solution.py:161
  2.0 18.4 %all-to-all-start = ((bf16[128,2,1280]{2,1,0:T(2,128)(2,1)}), bf16[128,2,1280]{2,1,0:T(2,128)(2,1)S(1)}, u32[]{:S(2)}, u32[]{:S(2)}) async-start(bf16[128,2,1280]{2,1,0:T(2,128)(2,1)} %bitcast.14), calls=%async_computation | async-start | bytes 1310720 | tf_op jit(solution)/shard_map/all_to_all | solution.py:312
  20.5 0.0 copy-start.2
  20.6 22.1 %all-to-all-done.table_ref = bf16[128,2,1280]{2,1,0:T(2,128)(2,1)S(1)} async-done(((bf16[128,2,1280]{2,1,0:T(2,128)(2,1)}), bf16[128,2,1280]{2,1,0:T(2,128)(2,1)S(1)}, u32[]{:S(2)}, u32[]{:S(2)}) %all-to-all-start) | async-done | bytes 655392 | tf_op jit(solution)/shard_map/all_to_all | solution.py:312
  42.7 0.1 dynamic-slice_bitcast_fusion
  42.8 0.1 reshape.23
  42.9 0.1 reshape.28.wanted_ref
  42.9 1.3 %shard_map.48 = bf16[4,8,128,128]{3,2,1,0:T(8,128)(2,1)} custom-call(s32[1,128]{1,0:T(1,128)S(1)} %reshape.28.wanted_ref, bf16[128,2,1280]{2,1,0:T(2,128)(2,1)S(1)} %all-to-all-done.table_ref), custom_call_target="tpu_custom_call" | custom-call | tf_op jit(solution)/shard_map/pallas_call | solution.py:280
  44.3 6.8 %all-to-all-start.1 = ((bf16[32,128,128]{2,1,0:T(8,128)(2,1)}), bf16[32,128,128]{2,1,0:T(8,128)(2,1)S(1)}, u32[]{:S(2)}, u32[]{:S(2)}) async-start(bf16[32,128,128]{2,1,0:T(8,128)(2,1)} %bitcast.3), calls=%async_computation.1 | async-start | bytes 2097152 | tf_op jit(solution)/shard_map/all_to_all | solution.py:326
  51.1 0.0 copy-done.2
  51.1 5.0 %shard_map.46 = (bf16[16,128,576]{2,1,0:T(8,128)(2,1)S(1)}, s32[2,1,512]{2,1,0:T(1,128)S(1)}, f32[2,32,1152]{2,1,0:T(8,128)S(1)}) custom-call(s32[2,8]{1,0:T(2,128)S(1)} %copy-done.2, bf16[16,576,128]{2,1,0:T(8,128)(2,1)} %bitcast.17, bf16[2,36864]{1,0:T(2,128)(2,1)} %latent_hbm.3), custom_call_target="tpu_custom_call" | custom-call | flops 1000000000 | bytes 10485760 | tf_op jit(solution)/shard_map/pallas_call | solution.py:225
  56.1 0.0 copy-start
  56.2 1.5 %copy-done = bf16[16,128,576]{2,1,0:T(8,128)(2,1)} copy-done((bf16[16,128,576]{2,1,0:T(8,128)(2,1)}, bf16[16,128,576]{2,1,0:T(8,128)(2,1)S(1)}, u32[]{:S(2)}) %copy-start) | copy-done | bytes 2359320
  57.7 10.2 %all-to-all-done.1.k_ref = bf16[32,128,128]{2,1,0:T(8,128)(2,1)S(1)} async-done(((bf16[32,128,128]{2,1,0:T(8,128)(2,1)}), bf16[32,128,128]{2,1,0:T(8,128)(2,1)S(1)}, u32[]{:S(2)}, u32[]{:S(2)}) %all-to-all-start.1) | async-done | bytes 1048608 | tf_op jit(solution)/shard_map/all_to_all | solution.py:326
  67.8 0.0 copy-start.1
  67.8 1.7 %copy-done.1 = bf16[16,128,576]{2,1,0:T(8,128)(2,1)S(1)} copy-done((bf16[16,128,576]{2,1,0:T(8,128)(2,1)S(1)}, bf16[16,128,576]{2,1,0:T(8,128)(2,1)}, u32[]{:S(2)}) %copy-start.1) | copy-done | bytes 2359320
  69.6 4.8 %shard_map.49 = bf16[128,2048]{1,0:T(8,128)(2,1)S(1)} custom-call(bf16[16,128,576]{2,1,0:T(8,128)(2,1)S(1)} %copy-done.1, bf16[32,128,128]{2,1,0:T(8,128)(2,1)S(1)} %all-to-all-done.1.k_ref, f32[2,32,1152]{2,1,0:T(8,128)S(1)} %get-tuple-element.9.own_ref, s32[2,1,512]{2,1,0:T(1,128)S(1)} %get-tuple-element.10.place_ref, bf16[16,512,128]{2,1,0:T(8,128)(2,1)} %w_hbm.1), custom_call_target="tpu_custom_call" | custom-call | tf_op jit(solution)/shard_map/pallas_call | solution.py:106
  74.4 12.0 %all_to_all.29 = bf16[4,32,2048]{2,1,0:T(8,128)(2,1)S(1)} all-to-all(bf16[4,32,2048]{2,1,0:T(8,128)(2,1)S(1)} %bitcast.13), channel_id=1, replica_groups=mesh['ctx'=128,'head'=4] {'head'}, dimensions={0} | all-to-all | bytes 1048576 | tf_op jit(solution)/shard_map/all_to_all | solution.py:335
  86.4 0.8 copy.9
  (2 shorter events, 0.1 us)
Async XLA Ops:
  2.0 40.6 %all-to-all-start = ((bf16[128,2,1280]{2,1,0:T(2,128)(2,1)}), bf16[128,2,1280]{2,1,0:T(2,128)(2,1)S(1)}, u32[]{:S(2)}, u32[]{:S(2)}) async-start(bf16[128,2,1280]{2,1,0:T(2,128)(2,1)} %bitcast.14), calls=%async_computation | async-start | bytes 1310720 | tf_op jit(solution)/shard_map/all_to_all | solution.py:312
  20.5 30.6 %copy-start.2 = (s32[2,8]{1,0:T(2,128)S(1)}, s32[2,8]{1,0:T(2,128)}, u32[]{:S(2)}) copy-start(s32[2,8]{1,0:T(2,128)} %selected_hbm.1) | copy-start | bytes 196
  44.3 23.6 %all-to-all-start.1 = ((bf16[32,128,128]{2,1,0:T(8,128)(2,1)}), bf16[32,128,128]{2,1,0:T(8,128)(2,1)S(1)}, u32[]{:S(2)}, u32[]{:S(2)}) async-start(bf16[32,128,128]{2,1,0:T(8,128)(2,1)} %bitcast.3), calls=%async_computation.1 | async-start | bytes 2097152 | tf_op jit(solution)/shard_map/all_to_all | solution.py:326
  56.1 1.5 %copy-start = (bf16[16,128,576]{2,1,0:T(8,128)(2,1)}, bf16[16,128,576]{2,1,0:T(8,128)(2,1)S(1)}, u32[]{:S(2)}) copy-start(bf16[16,128,576]{2,1,0:T(8,128)(2,1)S(1)} %get-tuple-element.8.q_ref) | copy-start | bytes 7077892
  67.8 1.7 %copy-start.1 = (bf16[16,128,576]{2,1,0:T(8,128)(2,1)S(1)}, bf16[16,128,576]{2,1,0:T(8,128)(2,1)}, u32[]{:S(2)}) copy-start(bf16[16,128,576]{2,1,0:T(8,128)(2,1)} %copy-done) | copy-start | bytes 7077892
